TPU v7x, 32 devices: a whole 2x2x4 slice. The times are simulated.
32 devices in a mesh: section: 4 (over y, x), dev: 8 (over z, core).
Axes of the slice: x: 2, y: 2, z: 4, core: 2. Of those that a mesh axis runs over, the one named last changes fastest.
Arguments:
- hidden: bfloat16 [256, 2048], P('dev'), may hold values from -8 to 8
- lengths: int32 [256], P('dev'), may hold values from 1 to 256, as said below
- attn_gain: float32 [2048], replicated, may hold values from 0.1 to 1.9
- w_query: bfloat16 [2048, 3072], P(None, 'section'), may hold values from -0.125 to 0.125
- w_latent: bfloat16 [2048, 512], replicated, may hold values from -0.125 to 0.125
- latent_gain: float32 [512], replicated, may hold values from 0.1 to 1.9
- w_rope_key: bfloat16 [64, 2048], replicated, may hold values from -0.125 to 0.125
- w_key_up: bfloat16 [16, 512, 128], P('section'), may hold values from -0.5 to 0.5
- w_value_up: bfloat16 [16, 512, 128], P('section'), may hold values from -0.25 to 0.25
- w_out: bfloat16 [2048, 2048], P('section'), may hold values from -0.125 to 0.125
- latent_cache: bfloat16 [256, 256, 512], P('dev'), may hold values from -6 to 6
- rope_cache: bfloat16 [256, 64, 256], P('dev'), may hold values from -1200 to 1200
- ffn_gain: float32 [2048], replicated, may hold values from 0.1 to 1.9
- expert_ids: int32 [256, 6], P('dev'), may hold values from 0 to 63, all different within a row; in each aligned block of 8 rows (0 to 7, 8 to 15, ...) at most 2 rows name the same one
- route_weights: float32 [256, 6], P('dev'), may hold values from 0.05 to 0.5
- w_gate_up: bfloat16 [64, 2, 1408, 2048], P('dev', None, 'section'), may hold values from -0.125 to 0.125
- w_down: bfloat16 [64, 1408, 2048], P('dev', 'section'), may hold values from -0.15625 to 0.15625
Outputs:
- layer_out: bfloat16 [256, 2048], P('dev')
Inputs may be any that keep to these rules, and one draw needn't show every extreme that they name: `lengths`: every aligned block of 32 rows holds a row of length 256. `expert_ids`: each row names 6 different experts. In every aligned block of 8 rows no expert is named by more than 2 rows, and some block has an expert named by exactly 2.
All inputs are finite; a program needn't handle non-finite values.
Results may differ from a plain program's by a relative error of at most 0.011.
Values may be sent and summed in bfloat16 or wider, within the bound.
A program may use at most 128 MiB of HBM per device.

v0:
```python
import functools

import jax
import jax.numpy as jnp
from jax import lax
from jax.experimental import pallas as pl
from jax.experimental.pallas import tpu as pltpu
from jax.sharding import PartitionSpec as P

MOST = 2
MESH = pl.DeviceIdType.MESH


epsilon = 1e-06
far_below = -1e30


def rms_norm(values, norm_gain):
    mean_square = jnp.mean(values * values, axis=-1, keepdims=True)
    return values * lax.rsqrt(mean_square + epsilon) * norm_gain


def rotary(values, positions):
    half_width = values.shape[-1] // 2
    step_index = jnp.arange(half_width, dtype=jnp.float32)
    frequency = jnp.exp(-jnp.log(10000.0) * step_index / half_width)
    angles = positions.astype(jnp.float32)[:, None] * frequency[None, :]
    if values.ndim == 3:
        angles = angles[:, None, :]
    cosine = jnp.cos(angles)
    sine_part = jnp.sin(angles)
    first_half = values[..., :half_width]
    second = values[..., half_width:]
    return jnp.concatenate(
        [first_half * cosine - second * sine_part, second * cosine + first_half * sine_part],
        axis=-1,
    )


def route_table(own_ids, own_weights, experts, block_index):
    hit = own_ids[:, :, None] == jnp.arange(experts, dtype=jnp.int32)[None, None, :]
    dense = jnp.sum(jnp.where(hit, own_weights[:, :, None], 0.0), axis=1)
    routed = jnp.any(hit, axis=1).astype(jnp.int32)
    rank = jnp.cumsum(routed, axis=0) - routed
    slot = jnp.where(routed > 0, block_index * MOST + rank, -1)
    return jnp.concatenate([dense, slot.astype(jnp.float32)], axis=1)


def expert_kernel(
    sections,
    devices,
    part_ref,
    hidden_ref,
    gain_ref,
    table_ref,
    w_up_ref,
    w_down_ref,
    out_ref,
    w_up,
    w_down,
    part_in,
    middle,
    row_out,
    rows_all,
    tables,
    pick,
    mix,
    packed,
    expert_out,
    sum_out,
    sum_in,
    pair_in,
    pair_sum,
    own_out,
    finished,
    up_sem,
    down_sem,
    part_send,
    part_recv,
    table_send,
    table_recv,
    row_send,
    row_recv,
    sum_send,
    sum_recv,
    pair_send,
    pair_recv,
    done_send,
    done_recv,
):
    section = lax.axis_index("section")
    dev = lax.axis_index("dev")
    total = sections * devices
    me = dev * sections + section
    local = w_up.shape[0]
    rows = total * row_out.shape[0]
    width = row_out.shape[1]
    experts = tables.shape[2] // 2
    slots = packed.shape[0] // local
    f32 = jnp.float32

    def up_copy(e):
        return pltpu.make_async_copy(w_up_ref.at[e], w_up.at[e], up_sem.at[e])

    def down_copy(e):
        return pltpu.make_async_copy(w_down_ref.at[e], w_down.at[e], down_sem.at[e])

    def place(t):
        return (lax.rem(t, sections), t // sections)

    def to_all(source, landing, send_sem, recv_sem):
        def copy(i, here):
            t = lax.rem(me + i, total)
            return pltpu.make_async_remote_copy(
                src_ref=source(t),
                dst_ref=landing.at[here],
                send_sem=send_sem.at[i],
                recv_sem=recv_sem.at[here],
                device_id=place(t),
                device_id_type=MESH,
            )

        @pl.loop(1, total)
        def _(i):
            copy(i, me).start()

        def wait_recv():
            @pl.loop(1, total)
            def _(i):
                copy(i, lax.rem(me + i, total)).wait_recv()

        def wait_send():
            @pl.loop(1, total)
            def _(i):
                copy(i, me).wait_send()

        return wait_recv, wait_send

    def to_sections(source, landing, send_sem, recv_sem):
        def copy(i, here):
            t = lax.rem(section + i, sections)
            return pltpu.make_async_remote_copy(
                src_ref=source(t),
                dst_ref=landing.at[here],
                send_sem=send_sem.at[i],
                recv_sem=recv_sem.at[here],
                device_id=(t, dev),
                device_id_type=MESH,
            )

        for i in range(1, sections):
            copy(i, section).start()

        def wait_recv():
            for i in range(1, sections):
                copy(i, lax.rem(section + i, sections)).wait_recv()

        def wait_send():
            for i in range(1, sections):
                copy(i, section).wait_send()

        return wait_recv, wait_send

    @pl.loop(0, local)
    def _(e):
        up_copy(e).start()
        down_copy(e).start()

    barrier = pltpu.get_barrier_semaphore()

    @pl.loop(1, total)
    def _(i):
        pl.semaphore_signal(
            barrier, inc=1, device_id=place(lax.rem(me + i, total)), device_id_type=MESH
        )

    pl.semaphore_wait(barrier, total - 1)

    part_recv_all, part_send_all = to_sections(
        lambda t: part_ref.at[t], part_in, part_send, part_recv
    )
    table_recv_all, table_send_all = to_all(lambda t: table_ref, tables, table_send, table_recv)
    part_in[section] = part_ref[section]
    tables[me] = table_ref[...]
    part_recv_all()
    summed = part_in[0]
    for j in range(1, sections):
        summed = summed + part_in[j]
    middle_rows = (hidden_ref[...].astype(f32) + summed).astype(jnp.bfloat16).astype(f32)
    middle[...] = middle_rows
    normed_rows = rms_norm(middle_rows, gain_ref[...]).astype(jnp.bfloat16)
    row_out[...] = normed_rows
    rows_all[me] = normed_rows
    row_recv_all, row_send_all = to_all(lambda t: row_out, rows_all, row_send, row_recv)

    table_recv_all()
    table = tables[...].reshape(rows, 2 * experts)
    lane = lax.broadcasted_iota(jnp.int32, (rows, 2 * experts), 1)
    column = lax.broadcasted_iota(jnp.int32, (rows, local * slots), 1)
    slot_at = jnp.full((rows, local * slots), -1.0, f32)
    weight_at = jnp.zeros((rows, local * slots), f32)
    for e in range(local):
        expert = dev * local + e
        weight_col = jnp.sum(jnp.where(lane == expert, table, 0.0), axis=1, keepdims=True)
        slot_col = jnp.sum(jnp.where(lane == experts + expert, table, 0.0), axis=1, keepdims=True)
        slot_col = jnp.where(slot_col < 0.0, -1.0, slot_col + float(e * slots))
        inside = (column >= e * slots) & (column < (e + 1) * slots)
        slot_at = jnp.where(inside, slot_col, slot_at)
        weight_at = jnp.where(inside, weight_col, weight_at)
    chosen = column.astype(f32) == slot_at
    pick[...] = jnp.where(chosen, 1.0, 0.0).astype(jnp.bfloat16)
    mix[...] = jnp.where(chosen, weight_at, 0.0).astype(jnp.bfloat16)

    row_recv_all()
    tile = 512

    @pl.loop(0, width // tile)
    def _(c):
        span = pl.ds(pl.multiple_of(c * tile, tile), tile)
        block = rows_all[:, :, span].astype(f32).reshape(rows, tile).astype(jnp.bfloat16)
        packed[:, span] = lax.dot_general(
            pick[...], block, (((0,), (0,)), ((), ())), preferred_element_type=f32
        ).astype(jnp.bfloat16)

    @pl.loop(0, local)
    def _(e):
        span = pl.ds(pl.multiple_of(e * slots, slots), slots)
        up_copy(e).wait()
        slot_rows = packed[span, :]
        flat = (((1,), (1,)), ((), ()))
        gate = lax.dot_general(slot_rows, w_up[e, 0], flat, preferred_element_type=f32)
        lift = lax.dot_general(slot_rows, w_up[e, 1], flat, preferred_element_type=f32)
        activated = (gate / (1.0 + jnp.exp(-gate)) * lift).astype(jnp.bfloat16)
        down_copy(e).wait()
        expert_out[span, :] = jnp.dot(
            activated, w_down[e], preferred_element_type=f32
        ).astype(jnp.bfloat16)

    @pl.loop(0, width // tile)
    def _(c):
        span = pl.ds(pl.multiple_of(c * tile, tile), tile)
        mixed = jnp.dot(mix[...], expert_out[:, span], preferred_element_type=f32)
        sum_out[:, :, span] = mixed.reshape(total, rows // total, tile).astype(jnp.bfloat16)

    core = lax.rem(dev, 2)
    pairs = devices // 2
    own_pair = dev // 2
    partner = (section, dev + 1 - 2 * core)

    def pair_copy(k):
        z = lax.rem(own_pair + 1 + k, pairs)
        source = (2 * z + 1 - core) * sections
        return pltpu.make_async_remote_copy(
            src_ref=sum_out.at[pl.ds(source, sections)],
            dst_ref=pair_in.at[z],
            send_sem=pair_send.at[k],
            recv_sem=pair_recv.at[k],
            device_id=partner,
            device_id_type=MESH,
        )

    def block_copy(z, t, here, slot):
        return pltpu.make_async_remote_copy(
            src_ref=pair_sum.at[z, t],
            dst_ref=sum_in.at[here],
            send_sem=sum_send.at[slot],
            recv_sem=sum_recv.at[here],
            device_id=(t, 2 * z + core),
            device_id_type=MESH,
        )

    here = own_pair * sections + section

    @pl.loop(0, pairs)
    def _(k):
        pair_copy(k).start()

    def add_pair(k):
        z = lax.rem(own_pair + 1 + k, pairs)
        pair_copy(k).wait_recv()
        mine = sum_out[pl.ds((2 * z + core) * sections, sections)].astype(f32)
        pair_sum[z] = (mine + pair_in[z].astype(f32)).astype(jnp.bfloat16)
        return z

    @pl.loop(0, pairs - 1)
    def _(k):
        z = add_pair(k)

        @pl.loop(0, sections)
        def _(j):
            t = lax.rem(section + j, sections)
            block_copy(z, t, here, z * sections + t).start()

    add_pair(pairs - 1)

    @pl.loop(1, sections)
    def _(j):
        t = lax.rem(section + j, sections)
        block_copy(own_pair, t, here, own_pair * sections + t).start()

    sum_in[here] = pair_sum[own_pair, section]
    part_send_all()
    table_send_all()
    row_send_all()
    half = pairs * sections

    @pl.loop(1, half)
    def _(i):
        t = lax.rem(here + i, half)
        block_copy(t // sections, lax.rem(t, sections), t, t).wait_recv()

    result = (middle[...] + jnp.sum(sum_in[...].astype(f32), axis=0)).astype(jnp.bfloat16)
    own_out[...] = result
    finished[section] = result
    done_recv_all, done_send_all = to_sections(
        lambda t: own_out, finished, done_send, done_recv
    )

    @pl.loop(1, half)
    def _(i):
        t = lax.rem(here + i, half)
        block_copy(t // sections, lax.rem(t, sections), here, t).wait_send()

    @pl.loop(0, pairs)
    def _(k):
        pair_copy(k).wait_send()

    done_recv_all()
    out_ref[...] = finished[...]
    done_send_all()


def expert_layer(part, own_hidden, ffn_gain, table, w_gate_up, w_down):
    sections = lax.axis_size("section")
    devices = lax.axis_size("dev")
    total = sections * devices
    quarter, width = own_hidden.shape
    local, _, units, _ = w_gate_up.shape
    slots = total * MOST
    rows = total * quarter
    bf16, f32 = jnp.bfloat16, jnp.float32
    vmem = pl.BlockSpec(memory_space=pltpu.VMEM)
    anywhere = pl.BlockSpec(memory_space=pl.ANY)
    sems = lambda count: pltpu.SemaphoreType.DMA((count,))
    out = pl.pallas_call(
        functools.partial(expert_kernel, sections, devices),
        out_shape=jax.ShapeDtypeStruct((sections, quarter, width), bf16),
        in_specs=[vmem] * 4 + [anywhere] * 2,
        out_specs=vmem,
        scratch_shapes=[
            pltpu.VMEM(w_gate_up.shape, bf16),
            pltpu.VMEM(w_down.shape, bf16),
            pltpu.VMEM((sections, quarter, width), f32),
            pltpu.VMEM((quarter, width), f32),
            pltpu.VMEM((quarter, width), bf16),
            pltpu.VMEM((total, quarter, width), bf16),
            pltpu.VMEM((total,) + table.shape, f32),
            pltpu.VMEM((rows, local * slots), bf16),
            pltpu.VMEM((rows, local * slots), bf16),
            pltpu.VMEM((local * slots, width), bf16),
            pltpu.VMEM((local * slots, width), bf16),
            pltpu.VMEM((total, quarter, width), bf16),
            pltpu.VMEM((total // 2, quarter, width), bf16),
            pltpu.VMEM((devices // 2, sections, quarter, width), bf16),
            pltpu.VMEM((devices // 2, sections, quarter, width), bf16),
            pltpu.VMEM((quarter, width), bf16),
            pltpu.VMEM((sections, quarter, width), bf16),
            sems(local),
            sems(local),
            sems(sections),
            sems(sections),
            sems(total),
            sems(total),
            sems(total),
            sems(total),
            sems(total // 2),
            sems(total // 2),
            sems(devices // 2),
            sems(devices // 2),
            sems(sections),
            sems(sections),
        ],
        compiler_params=pltpu.CompilerParams(
            collective_id=0, has_side_effects=True, vmem_limit_bytes=58 * 1024 * 1024
        ),
    )(
        part.reshape(sections, quarter, width),
        own_hidden,
        ffn_gain.reshape(1, width),
        table,
        w_gate_up,
        w_down,
    )
    return out.reshape(sections * quarter, width)


def attend(
    query_latent, query_rope, latent_new, key_new, latent_cache, rope_cache, lengths, score_scale
):
    scores = jnp.einsum(
        "rhl,rtl->rht", query_latent, latent_cache, preferred_element_type=jnp.float32
    )
    scores = scores + jnp.einsum(
        "rhp,rpt->rht", query_rope, rope_cache, preferred_element_type=jnp.float32
    )
    scores = scores * score_scale
    self_score = jnp.einsum(
        "rhl,rl->rh", query_latent, latent_new, preferred_element_type=jnp.float32
    )
    self_score = (
        self_score
        + jnp.einsum("rhp,rp->rh", query_rope, key_new, preferred_element_type=jnp.float32)
    ) * score_scale
    places = jnp.arange(latent_cache.shape[1], dtype=jnp.int32)
    valid_mask = places[None, None, :] < lengths[:, None, None]
    masked = jnp.where(valid_mask, scores, far_below)
    peak_score = jnp.maximum(jnp.max(masked, axis=2), self_score)
    weights = jnp.where(valid_mask, jnp.exp(masked - peak_score[:, :, None]), 0.0)
    self_weight = jnp.exp(self_score - peak_score)
    totals = jnp.sum(weights, axis=2) + self_weight
    prob_cache = (weights / totals[:, :, None]).astype(jnp.bfloat16)
    prob_self = (self_weight / totals).astype(jnp.bfloat16)
    mixed = jnp.einsum("rht,rtl->rhl", prob_cache, latent_cache, preferred_element_type=jnp.float32)
    mixed = (
        mixed
        + prob_self.astype(jnp.float32)[:, :, None] * latent_new.astype(jnp.float32)[:, None, :]
    )
    return mixed.astype(jnp.bfloat16)


def per_device(
    hidden,
    lengths,
    attn_gain,
    w_query,
    w_latent,
    latent_gain,
    w_rope_key,
    w_key_up,
    w_value_up,
    w_out,
    latent_cache,
    rope_cache,
    ffn_gain,
    expert_ids,
    route_weights,
    w_gate_up,
    w_down,
):
    sections = lax.axis_size("section")
    devices = lax.axis_size("dev")
    row_count = hidden.shape[0]
    quarter = row_count // sections
    head_local = w_key_up.shape[0]
    nope_width = w_key_up.shape[2]
    rope_width = w_rope_key.shape[0]
    score_scale = (nope_width + rope_width) ** (-0.5)
    normed = rms_norm(hidden.astype(jnp.float32), attn_gain).astype(jnp.bfloat16)
    queries = jnp.dot(normed, w_query, preferred_element_type=jnp.float32).astype(jnp.bfloat16)
    queries = queries.reshape(row_count, head_local, nope_width + rope_width)
    query_rope = rotary(queries[:, :, nope_width:].astype(jnp.float32), lengths).astype(
        jnp.bfloat16
    )
    query_latent = jnp.einsum(
        "rhn,hln->rhl", queries[:, :, :nope_width], w_key_up, preferred_element_type=jnp.float32
    ).astype(jnp.bfloat16)
    latent_new = rms_norm(
        jnp.dot(normed, w_latent, preferred_element_type=jnp.float32), latent_gain
    ).astype(jnp.bfloat16)
    key_raw = lax.dot_general(
        normed, w_rope_key, (((1,), (1,)), ((), ())), preferred_element_type=jnp.float32
    )
    key_new = rotary(key_raw, lengths).astype(jnp.bfloat16)
    mixed_latent = attend(
        query_latent,
        query_rope,
        latent_new,
        key_new,
        latent_cache,
        rope_cache,
        lengths,
        score_scale,
    )
    head_out = jnp.einsum(
        "rhl,hlv->rhv", mixed_latent, w_value_up, preferred_element_type=jnp.float32
    ).astype(jnp.bfloat16)
    heads_flat = head_out.reshape(row_count, -1)
    section_index = lax.axis_index("section")
    first_row = section_index * quarter
    own_hidden = lax.dynamic_slice_in_dim(hidden, first_row, quarter, 0)
    own_ids = lax.dynamic_slice_in_dim(expert_ids, first_row, quarter, 0)
    own_weights = lax.dynamic_slice_in_dim(route_weights, first_row, quarter, 0)
    block_index = lax.axis_index("dev") * sections + section_index
    table = route_table(own_ids, own_weights, w_gate_up.shape[0] * devices, block_index)
    part = jnp.dot(heads_flat, w_out, preferred_element_type=jnp.float32)
    return expert_layer(part, own_hidden, ffn_gain, table, w_gate_up, w_down)


def solution(mesh):
    in_specs = (
        P("dev", None),
        P("dev"),
        P(),
        P(None, "section"),
        P(),
        P(),
        P(),
        P("section", None, None),
        P("section", None, None),
        P("section", None),
        P("dev", None, None),
        P("dev", None, None),
        P(),
        P("dev", None),
        P("dev", None),
        P("dev", None, "section", None),
        P("dev", "section", None),
    )
    out_specs = P("dev", None)
    return jax.shard_map(
        per_device, mesh=mesh, in_specs=in_specs, out_specs=out_specs, check_vma=False
    )
```

profile of v0, /device:TPU:0, one launch (start us, length us, event | category | flops | bytes accessed | tf_op | source)
XLA Modules:
  0.0 96.1 jit_solution(787043451751886461)
XLA Ops:
  0.0 0.0 copy-start
  0.0 0.8 convert_element_type.60
  0.8 1.2 %fusion.7 = f32[32]{0:T(128)S(1)} fusion(bf16[32,2048]{1,0:T(8,128)(2,1)} %param.17), kind=kLoop, calls=%fused_computation.14 | loop fusion | flops 196576 | bytes 131200 | tf_op jit(solution)/shard_map/reduce_sum | solution.py:19
  2.1 0.8 constant_dynamic-slice_fusion.1
  2.8 0.1 fusion.21
  3.0 0.8 constant_dynamic-slice_fusion
  3.7 0.1 select_reduce_fusion
  3.8 0.7 pad_maximum_fusion.1.table_ref
  4.5 0.7 iota_compare_fusion
  5.2 1.3 %fusion.31 = f32[32,64]{1,0:T(8,128)S(1)} fusion(bf16[64,2048]{1,0:T(8,128)(2,1)} %param.23, bf16[32,2048]{1,0:T(8,128)(2,1)} %param.17, f32[2048]{0:T(1024)} %param.19, f32[32]{0:T(128)S(1)} %add_rsqrt_fusion.1), kind=kOutput, calls=%fused_computation.65 | convolution fusion | flops 8650752 | bytes 409728 | tf_op jit(solution)/shard_map/dot_general | solution.py:470
  6.5 0.2 subtract_convert_fusion.1
  6.7 0.1 maximum_bitcast_fusion
  6.7 1.4 %constant_dynamic-slice_fusion.2.hidden_ref = bf16[8,2048]{1,0:T(8,128)(2,1)} fusion(bf16[32,2048]{1,0:T(8,128)(2,1)} %param.17, s32[]{:T(128)S(6)} %select_n.22), kind=kLoop, calls=%fused_computation.56 | loop fusion | bytes 65540 | tf_op jit(solution)/shard_map/dynamic_slice | solution.py:490
  8.1 0.0 copy-done
  8.1 1.6 %convolution_convert_fusion.1 = bf16[32,768]{1,0:T(8,128)(2,1)S(1)} fusion(bf16[2048,768]{1,0:T(8,128)(2,1)S(1)} %copy-done, bf16[32,2048]{1,0:T(8,128)(2,1)} %param.17, f32[2048]{0:T(1024)} %param.19, f32[32]{0:T(128)S(1)} %add_rsqrt_fusion.1), kind=kOutput, calls=%fused_computation.9 | convolution fusion | flops 100950016 | bytes 3334272 | tf_op jit(solution)/shard_map/dot_general | solution.py:459
  9.7 0.1 reshape.110
  9.9 0.0 copy-start.2
  9.9 0.1 subtract_convert_fusion
  10.0 0.2 fusion.22
  10.2 1.5 %fusion.28 = f32[32,4,256]{2,1,0:T(4,128)S(1)} fusion(bf16[32,64,256]{2,1,0:T(8,128)(2,1)} %param.28, bf16[32,4,32]{2,1,0:T(4,128)(2,1)S(1)} %get-tuple-element.6, bf16[32,4,32]{2,1,0:T(4,128)(2,1)S(1)} %get-tuple-element.5), kind=kOutput, calls=%fused_computation.62 | convolution fusion | flops 4227072 | bytes 1196032 | tf_op jit(solution)/shard_map/rhp,rpt->rht/dot_general | solution.py:403
  11.8 2.2 %multiply_reduce_fusion = (f32[32]{0:T(128)S(1)}, f32[32,512]{1,0:T(8,128)S(1)}) fusion(bf16[2048,512]{1,0:T(8,128)(2,1)} %param.21, bf16[32,2048]{1,0:T(8,128)(2,1)S(1)} %copy-done.1, f32[2048]{0:T(1024)S(1)} %copy-done.4, f32[32]{0:T(128)S(1)} %add_rsqrt_fusion.1), kind=kOutput, calls=%fused_computation.28 | convolution fusion | flops 67403744 | bytes 2302208 | tf_op jit(solution)/shard_map/dot_general | solution.py:468
  14.0 0.1 fusion.30
  14.1 0.3 fusion.3
  14.4 0.3 fusion.11
  14.7 5.7 %fusion.36 = (f32[32,4]{1,0:T(8,128)S(1)}, f32[32,4,256]{2,1,0:T(4,128)S(1)}) fusion(f32[32,4,256]{2,1,0:T(4,128)S(1)} %fusion.28, bf16[32,256,512]{2,1,0:T(8,128)(2,1)} %param.27, bf16[32,4,512]{2,0,1:T(8,128)(2,1)S(1)} %fusion.3, pred[32,256]{1,0:T(8,128)(4,1)S(1)} %iota_compare_fusion), kind=kOutput, calls=%fused_computation.67 | convolution fusion | flops 33685376 | bytes 8790528 | tf_op jit(solution)/shard_map/rhl,rtl->rht/dot_general | solution.py:400
  20.4 0.2 fusion.14
  20.7 0.0 copy-start.3
  20.7 4.7 %fusion.2 = bf16[32,4,512]{2,1,0:T(4,128)(2,1)S(1)} fusion(bf16[32,256,512]{2,1,0:T(8,128)(2,1)} %param.27, f32[32,512]{1,0:T(8,128)S(1)} %get-tuple-element.8, f32[32,4]{1,0:T(8,128)S(1)} %get-tuple-element.10, f32[32,4,256]{2,1,0:T(4,128)S(1)} %get-tuple-element.18, f32[32,4]{1,0:T(8,128)S(1)} %get-tuple-element.9, f32[32,4]{1,0:T(8,128)S(1)} %fusion.25, ...), kind=kOutput, calls=%fused_computation.3 | convolution fusion | flops 33882112 | bytes 8726016 | tf_op jit(solution)/shard_map/rht,rtl->rhl/dot_general | solution.py:423
  25.3 0.2 fusion.6
  25.6 2.7 %fusion.part_ref = f32[4,8,2048]{2,1,0:T(8,128)} fusion(bf16[4,8,512]{2,1,0:T(8,128)(2,1)S(1)} %dot_general.45, bf16[512,2048]{1,0:T(8,128)(2,1)} %param.26), kind=kOutput, calls=%fused_computation | convolution fusion | flops 67108864 | bytes 2392064 | tf_op jit(solution)/shard_map/dot_general | solution.py:495
  28.4 66.1 %shard_map.163 = bf16[4,8,2048]{2,1,0:T(8,128)(2,1)} custom-call(f32[4,8,2048]{2,1,0:T(8,128)} %fusion.part_ref, bf16[8,2048]{1,0:T(8,128)(2,1)} %constant_dynamic-slice_fusion.2.hidden_ref, f32[1,2048]{1,0:T(1,128)} %bitcast.31, f32[8,128]{1,0:T(8,128)} %pad_maximum_fusion.1.table_ref, bf16[8,2,352,2048]{3,2,1,0:T(8,128)(2,1)} %w_up_ref.1, ...), custom_call_target="tpu_custom_call" | custom-call | tf_op jit(solution)/shard_map/pallas_call | solution.py:345
  94.5 1.6 %copy.53 = bf16[32,2048]{1,0:T(8,128)(2,1)} copy(bf16[32,2048]{1,0:T(8,128)(2,1)} %bitcast.26) | data formatting | bytes 262144
  (20 shorter events, 0.2 us)
Async XLA Ops:
  0.0 8.1 %copy-start = (bf16[2048,768]{1,0:T(8,128)(2,1)S(1)}, bf16[2048,768]{1,0:T(8,128)(2,1)}, u32[]{:S(2)}) copy-start(bf16[2048,768]{1,0:T(8,128)(2,1)} %param.20) | copy-start | bytes 9437188
  0.0 11.8 %copy-start.1 = (bf16[32,2048]{1,0:T(8,128)(2,1)S(1)}, bf16[32,2048]{1,0:T(8,128)(2,1)}, u32[]{:S(2)}) copy-start(bf16[32,2048]{1,0:T(8,128)(2,1)} %param.17) | copy-start | bytes 393220
  0.0 11.8 %copy-start.4 = (f32[2048]{0:T(1024)S(1)}, f32[2048]{0:T(1024)}, u32[]{:S(2)}) copy-start(f32[2048]{0:T(1024)} %param.19) | copy-start | bytes 24580
  8.1 5.9 %copy-start.5 = (f32[512]{0:T(512)S(1)}, f32[512]{0:T(512)}, u32[]{:S(2)}) copy-start(f32[512]{0:T(512)} %param.22) | copy-start | bytes 6148
  9.9 4.3 %copy-start.2 = (bf16[4,512,128]{2,1,0:T(8,128)(2,1)S(1)}, bf16[4,512,128]{2,1,0:T(8,128)(2,1)}, u32[]{:S(2)}) copy-start(bf16[4,512,128]{2,1,0:T(8,128)(2,1)} %param.24) | copy-start | bytes 1572868
  20.7 4.7 %copy-start.3 = (bf16[4,512,128]{2,1,0:T(8,128)(2,1)S(1)}, bf16[4,512,128]{2,1,0:T(8,128)(2,1)}, u32[]{:S(2)}) copy-start(bf16[4,512,128]{2,1,0:T(8,128)(2,1)} %param.25) | copy-start | bytes 1572868
where the time goes:
time: 97.1 us; the launch traced here: 96.1 us
  Pallas kernels  66.1 us (68%)
  matrix products  20.8 us (21%)
  local copies, waits for them, and re-layouts  4.68 us (5%)
  other arithmetic  4.33 us (4%)
    pallas_call x1, Pallas kernels, expert_layer(): pl.pallas_call(functools.partial(expert_kernel, sections, devices), out_s...  66.1 us
    dot_general x1, matrix products, attend(): jnp.einsum('rhl,rtl->rht', query_latent, latent_cache, preferred_element_...  5.74 us
    dot_general x1, matrix products, attend(): jnp.einsum('rht,rtl->rhl', prob_cache, latent_cache, preferred_element_ty...  4.68 us
    dot_general x1, matrix products, per_device(): part = jnp.dot(heads_flat, w_out, preferred_element_type=jnp.float32)  2.74 us
    dot_general x1, matrix products, per_device(): jnp.dot(normed, w_latent, preferred_element_type=jnp.float32)  2.22 us

commit v1 on v0

v1 whole, which is shorter than its diff:
```python
import functools

import jax
import jax.numpy as jnp
from jax import lax
from jax.experimental import pallas as pl
from jax.experimental.pallas import tpu as pltpu
from jax.sharding import PartitionSpec as P

MOST = 2
CHUNKS = 4
MESH = pl.DeviceIdType.MESH


epsilon = 1e-06
far_below = -1e30


def rms_norm(values, norm_gain):
    mean_square = jnp.mean(values * values, axis=-1, keepdims=True)
    return values * lax.rsqrt(mean_square + epsilon) * norm_gain


def rotary(values, positions):
    half_width = values.shape[-1] // 2
    step_index = jnp.arange(half_width, dtype=jnp.float32)
    frequency = jnp.exp(-jnp.log(10000.0) * step_index / half_width)
    angles = positions.astype(jnp.float32)[:, None] * frequency[None, :]
    if values.ndim == 3:
        angles = angles[:, None, :]
    cosine = jnp.cos(angles)
    sine_part = jnp.sin(angles)
    first_half = values[..., :half_width]
    second = values[..., half_width:]
    return jnp.concatenate(
        [first_half * cosine - second * sine_part, second * cosine + first_half * sine_part],
        axis=-1,
    )


def route_rows(table_ref, ids, weights, experts, place):
    rows, top = ids.shape
    lane = lax.broadcasted_iota(jnp.int32, (rows, experts), 1)
    row = lax.broadcasted_iota(jnp.int32, (rows, experts), 0)
    dense = jnp.zeros((rows, experts), jnp.float32)
    routed = jnp.zeros((rows, experts), jnp.float32)
    for k in range(top):
        hit = lane == ids[:, k : k + 1]
        dense = dense + jnp.where(hit, weights[:, k : k + 1], 0.0)
        routed = routed + jnp.where(hit, 1.0, 0.0)
    rank = jnp.zeros((rows, experts), jnp.float32)
    for j in range(rows - 1):
        rank = rank + jnp.where(row > j, routed[j : j + 1, :], 0.0)
    first = (place * MOST).astype(jnp.float32)
    table_ref[:, :experts] = dense
    table_ref[:, experts:] = jnp.where(routed > 0.0, first + rank, -1.0)


def expert_kernel(
    sections,
    devices,
    part_ref,
    hidden_ref,
    gain_ref,
    ids_ref,
    weights_ref,
    w_up_ref,
    w_down_ref,
    out_ref,
    w_up,
    w_down,
    part_in,
    middle,
    table,
    tables,
    own,
    rows_all,
    pick,
    mix,
    packed,
    lifted,
    activated,
    sum_out,
    pair_in,
    pair_sum,
    plane_in,
    plane_sum,
    line_in,
    own_out,
    finished,
    up_sem,
    down_sem,
    part_send,
    part_recv,
    table_send,
    table_recv,
    line_send,
    line_recv,
    plane_send,
    plane_recv,
    pair_send,
    pair_recv,
    back_pair_send,
    back_pair_recv,
    back_plane_send,
    back_plane_recv,
    back_line_send,
    back_line_recv,
    done_send,
    done_recv,
):
    section = lax.axis_index("section")
    dev = lax.axis_index("dev")
    core = lax.rem(dev, 2)
    line = dev // 2
    pairs = devices // 2
    total = sections * devices
    me = dev * sections + section
    local, _, units, width = w_up.shape
    chunks, quarter, span = own.shape
    rows = total * quarter
    experts = tables.shape[-1] // 2
    slots = packed.shape[0] // local
    bf16, f32 = jnp.bfloat16, jnp.float32
    partner = (section, dev + 1 - 2 * core)

    def remote(source, landing, send, recv, device):
        return pltpu.make_async_remote_copy(
            src_ref=source,
            dst_ref=landing,
            send_sem=send,
            recv_sem=recv,
            device_id=device,
            device_id_type=MESH,
        )

    def up_copy(e):
        return pltpu.make_async_copy(w_up_ref.at[e], w_up.at[e], up_sem.at[e])

    def down_copy(e):
        return pltpu.make_async_copy(w_down_ref.at[e], w_down.at[e], down_sem.at[e])

    @pl.loop(0, local)
    def _(e):
        up_copy(e).start()

    @pl.loop(0, local)
    def _(e):
        down_copy(e).start()

    barrier = pltpu.get_barrier_semaphore()

    @pl.loop(1, total)
    def _(i):
        t = lax.rem(me + i, total)
        pl.semaphore_signal(
            barrier, inc=1, device_id=(lax.rem(t, sections), t // sections), device_id_type=MESH
        )

    pl.semaphore_wait(barrier, total - 1)

    def part_copy(i, here):
        t = lax.rem(section + i, sections)
        return remote(part_ref.at[t], part_in.at[here], part_send.at[i], part_recv.at[here], (t, dev))

    for i in range(1, sections):
        part_copy(i, section).start()

    def place_of(t):
        return (lax.rem(t // sections, 2) * sections + lax.rem(t, sections)) * pairs + t // (
            2 * sections
        )

    here = place_of(me)
    route_rows(table, ids_ref[section], weights_ref[section], experts, here)
    tables[here] = table[...]

    def table_copy(i, landing):
        t = lax.rem(me + i, total)
        return remote(
            table,
            tables.at[landing],
            table_send.at[i],
            table_recv.at[landing],
            (lax.rem(t, sections), t // sections),
        )

    @pl.loop(1, total)
    def _(i):
        table_copy(i, here).start()

    summed = hidden_ref[section].astype(f32) + part_ref[section].astype(f32)
    for i in range(1, sections):
        t = lax.rem(section + i, sections)
        part_copy(i, t).wait_recv()
        summed = summed + part_in[t].astype(f32)
    middle_rows = summed.astype(bf16).astype(f32)
    middle[...] = middle_rows
    normed = rms_norm(middle_rows, gain_ref[...]).astype(bf16)

    def line_copy(k, i, slot):
        t = lax.rem(line + i, pairs)
        return remote(
            own.at[k],
            rows_all.at[k, core, section, slot],
            line_send.at[k, i],
            line_recv.at[k, slot],
            (section, 2 * t + core),
        )

    def plane_copy(k, i, source):
        return remote(
            rows_all.at[k, core, source],
            rows_all.at[k, core, source],
            plane_send.at[k, i],
            plane_recv.at[k, source],
            (lax.rem(section + i, sections), dev),
        )

    def pair_copy(k, which):
        return remote(
            rows_all.at[k, which], rows_all.at[k, which], pair_send.at[k], pair_recv.at[k], partner
        )

    for k in range(chunks):
        own[k] = normed[:, k * span : (k + 1) * span]
        rows_all[k, core, section, line] = normed[:, k * span : (k + 1) * span]

        @pl.loop(1, pairs)
        def _(i):
            line_copy(k, i, line).start()

    for k in range(chunks):

        @pl.loop(1, pairs)
        def _(i):
            line_copy(k, i, lax.rem(line + i, pairs)).wait_recv()

        for i in range(1, sections):
            plane_copy(k, i, section).start()

    @pl.loop(1, total)
    def _(i):
        table_copy(i, place_of(lax.rem(me + i, total))).wait_recv()

    known = tables[...].reshape(rows, 2 * experts).astype(bf16)
    wide = local * slots
    column = lax.broadcasted_iota(jnp.int32, (2 * experts, wide), 1).astype(f32)
    column_expert = jnp.floor((column + 0.5) * (1.0 / slots))
    entry = lax.broadcasted_iota(jnp.int32, (2 * experts, wide), 0)
    entry = (entry - dev * local).astype(f32)
    weight_pick = jnp.where(entry == column_expert, 1.0, 0.0).astype(bf16)
    slot_pick = jnp.where(entry == column_expert + float(experts), 1.0, 0.0).astype(bf16)
    slot_map = jnp.dot(known, slot_pick, preferred_element_type=f32)
    weight_map = jnp.dot(known, weight_pick, preferred_element_type=f32)
    column = lax.broadcasted_iota(jnp.int32, (rows, wide), 1).astype(f32)
    chosen = slot_map == column - jnp.floor((column + 0.5) * (1.0 / slots)) * slots
    pick[...] = jnp.where(chosen, 1.0, 0.0).astype(bf16)
    mix[...] = jnp.where(chosen, weight_map, 0.0).astype(bf16)

    def to_partner(k):
        for i in range(1, sections):
            plane_copy(k, i, lax.rem(section + i, sections)).wait_recv()
        pair_copy(k, core).start()

    flat = (((1,), (1,)), ((), ()))
    to_partner(0)
    for k in range(chunks):
        if k + 1 < chunks:
            to_partner(k + 1)
        pair_copy(k, 1 - core).wait_recv()
        block = rows_all[k].astype(f32).reshape(rows, span).astype(bf16)
        packed[...] = lax.dot_general(
            pick[...], block, (((0,), (0,)), ((), ())), preferred_element_type=f32
        ).astype(bf16)
        for e in range(local):
            if k == 0:
                up_copy(e).wait()
            held = slice(e * slots, (e + 1) * slots)
            both = lax.dot_general(
                packed[held, :],
                w_up[e, :, :, k * span : (k + 1) * span].reshape(2 * units, span),
                flat,
                preferred_element_type=f32,
            )
            if k > 0:
                both = both + lifted[held, :]
            if k + 1 < chunks:
                lifted[held, :] = both
            else:
                gate, lift = both[:, :units], both[:, units:]
                activated[held, :] = (gate / (1.0 + jnp.exp(-gate)) * lift).astype(bf16)

    def back_pair_copy(k, which):
        return remote(
            sum_out.at[k, which], pair_in.at[k], back_pair_send.at[k], back_pair_recv.at[k], partner
        )

    def back_plane_copy(k, i, landing):
        t = lax.rem(section + i, sections)
        return remote(
            pair_sum.at[k, t],
            plane_in.at[k, landing],
            back_plane_send.at[k, i],
            back_plane_recv.at[k, landing],
            (t, dev),
        )

    def back_line_copy(k, i, landing):
        t = lax.rem(line + i, pairs)
        return remote(
            plane_sum.at[k, t],
            line_in.at[k, landing],
            back_line_send.at[k, i],
            back_line_recv.at[k, landing],
            (section, 2 * t + core),
        )

    def done_copy(k, i, landing):
        return remote(
            own_out.at[k],
            finished.at[k, landing],
            done_send.at[k, i],
            done_recv.at[k, landing],
            (lax.rem(section + i, sections), dev),
        )

    def over_plane(k):
        back_pair_copy(k, 1 - core).wait_recv()
        pair_sum[k] = (sum_out[k, core].astype(f32) + pair_in[k].astype(f32)).astype(bf16)
        for i in range(1, sections):
            back_plane_copy(k, i, section).start()

    def over_line(k):
        added = pair_sum[k, section].astype(f32)
        for i in range(1, sections):
            t = lax.rem(section + i, sections)
            back_plane_copy(k, i, t).wait_recv()
            added = added + plane_in[k, t].astype(f32)
        plane_sum[k] = added.astype(bf16)

        @pl.loop(1, pairs)
        def _(i):
            back_line_copy(k, i, line).start()

        line_in[k, line] = plane_sum[k, line]

    def over_sections(k):
        @pl.loop(1, pairs)
        def _(i):
            back_line_copy(k, i, lax.rem(line + i, pairs)).wait_recv()

        result = middle[:, k * span : (k + 1) * span] + jnp.sum(line_in[k].astype(f32), axis=0)
        own_out[k] = result.astype(bf16)
        finished[k, section] = result.astype(bf16)
        for i in range(1, sections):
            done_copy(k, i, section).start()

    for k in range(chunks):
        part_of = slice(k * span, (k + 1) * span)
        outs = []
        for e in range(local):
            if k == 0:
                down_copy(e).wait()
            held = slice(e * slots, (e + 1) * slots)
            outs.append(
                jnp.dot(
                    activated[held, :], w_down[e, :, part_of], preferred_element_type=f32
                ).astype(bf16)
            )
        mixed = jnp.dot(mix[...], jnp.concatenate(outs, axis=0), preferred_element_type=f32)
        sum_out[k] = mixed.reshape(2, sections, pairs, quarter, span).astype(bf16)
        back_pair_copy(k, 1 - core).start()
        if k > 0:
            over_plane(k - 1)
    over_plane(chunks - 1)
    for k in range(chunks):
        over_line(k)
    for k in range(chunks):
        over_sections(k)
    for k in range(chunks):
        for i in range(1, sections):
            done_copy(k, i, lax.rem(section + i, sections)).wait_recv()
        out_ref[:, :, k * span : (k + 1) * span] = finished[k]

    for i in range(1, sections):
        part_copy(i, section).wait_send()

    @pl.loop(1, total)
    def _(i):
        table_copy(i, here).wait_send()

    for k in range(chunks):

        @pl.loop(1, pairs)
        def _(i):
            line_copy(k, i, line).wait_send()
            back_line_copy(k, i, line).wait_send()

        for i in range(1, sections):
            plane_copy(k, i, section).wait_send()
            back_plane_copy(k, i, section).wait_send()
            done_copy(k, i, section).wait_send()
        pair_copy(k, core).wait_send()
        back_pair_copy(k, 1 - core).wait_send()


def expert_layer(part, hidden, ffn_gain, expert_ids, route_weights, w_gate_up, w_down):
    sections = lax.axis_size("section")
    devices = lax.axis_size("dev")
    total = sections * devices
    pairs = devices // 2
    row_count, width = hidden.shape
    quarter = row_count // sections
    local, _, units, _ = w_gate_up.shape
    experts = local * devices
    slots = total * MOST
    rows = total * quarter
    chunks = CHUNKS
    span = width // chunks
    bf16, f32 = jnp.bfloat16, jnp.float32
    vmem = pl.BlockSpec(memory_space=pltpu.VMEM)
    anywhere = pl.BlockSpec(memory_space=pl.ANY)
    sems = lambda *count: pltpu.SemaphoreType.DMA(count)
    out = pl.pallas_call(
        functools.partial(expert_kernel, sections, devices),
        out_shape=jax.ShapeDtypeStruct((sections, quarter, width), bf16),
        in_specs=[vmem] * 5 + [anywhere] * 2,
        out_specs=vmem,
        scratch_shapes=[
            pltpu.VMEM(w_gate_up.shape, bf16),
            pltpu.VMEM(w_down.shape, bf16),
            pltpu.VMEM((sections, quarter, width), bf16),
            pltpu.VMEM((quarter, width), f32),
            pltpu.VMEM((quarter, 2 * experts), f32),
            pltpu.VMEM((total, quarter, 2 * experts), f32),
            pltpu.VMEM((chunks, quarter, span), bf16),
            pltpu.VMEM((chunks, 2, sections, pairs, quarter, span), bf16),
            pltpu.VMEM((rows, local * slots), bf16),
            pltpu.VMEM((rows, local * slots), bf16),
            pltpu.VMEM((local * slots, span), bf16),
            pltpu.VMEM((local * slots, 2 * units), f32),
            pltpu.VMEM((local * slots, units), bf16),
            pltpu.VMEM((chunks, 2, sections, pairs, quarter, span), bf16),
            pltpu.VMEM((chunks, sections, pairs, quarter, span), bf16),
            pltpu.VMEM((chunks, sections, pairs, quarter, span), bf16),
            pltpu.VMEM((chunks, sections, pairs, quarter, span), bf16),
            pltpu.VMEM((chunks, pairs, quarter, span), bf16),
            pltpu.VMEM((chunks, pairs, quarter, span), bf16),
            pltpu.VMEM((chunks, quarter, span), bf16),
            pltpu.VMEM((chunks, sections, quarter, span), bf16),
            sems(local),
            sems(local),
            sems(sections),
            sems(sections),
            sems(total),
            sems(total),
            sems(chunks, pairs),
            sems(chunks, pairs),
            sems(chunks, sections),
            sems(chunks, sections),
            sems(chunks),
            sems(chunks),
            sems(chunks),
            sems(chunks),
            sems(chunks, sections),
            sems(chunks, sections),
            sems(chunks, pairs),
            sems(chunks, pairs),
            sems(chunks, sections),
            sems(chunks, sections),
        ],
        compiler_params=pltpu.CompilerParams(
            collective_id=0, has_side_effects=True, vmem_limit_bytes=62 * 1024 * 1024
        ),
    )(
        part.astype(bf16).reshape(sections, quarter, width),
        hidden.reshape(sections, quarter, width),
        ffn_gain.reshape(1, width),
        expert_ids.reshape(sections, quarter, -1),
        route_weights.reshape(sections, quarter, -1),
        w_gate_up,
        w_down,
    )
    return out.reshape(row_count, width)


def attend(
    query_latent, query_rope, latent_new, key_new, latent_cache, rope_cache, lengths, score_scale
):
    scores = jnp.einsum(
        "rhl,rtl->rht", query_latent, latent_cache, preferred_element_type=jnp.float32
    )
    scores = scores + jnp.einsum(
        "rhp,rpt->rht", query_rope, rope_cache, preferred_element_type=jnp.float32
    )
    scores = scores * score_scale
    self_score = jnp.einsum(
        "rhl,rl->rh", query_latent, latent_new, preferred_element_type=jnp.float32
    )
    self_score = (
        self_score
        + jnp.einsum("rhp,rp->rh", query_rope, key_new, preferred_element_type=jnp.float32)
    ) * score_scale
    places = jnp.arange(latent_cache.shape[1], dtype=jnp.int32)
    valid_mask = places[None, None, :] < lengths[:, None, None]
    masked = jnp.where(valid_mask, scores, far_below)
    peak_score = jnp.maximum(jnp.max(masked, axis=2), self_score)
    weights = jnp.where(valid_mask, jnp.exp(masked - peak_score[:, :, None]), 0.0)
    self_weight = jnp.exp(self_score - peak_score)
    totals = jnp.sum(weights, axis=2) + self_weight
    prob_cache = (weights / totals[:, :, None]).astype(jnp.bfloat16)
    prob_self = (self_weight / totals).astype(jnp.bfloat16)
    mixed = jnp.einsum("rht,rtl->rhl", prob_cache, latent_cache, preferred_element_type=jnp.float32)
    mixed = (
        mixed
        + prob_self.astype(jnp.float32)[:, :, None] * latent_new.astype(jnp.float32)[:, None, :]
    )
    return mixed.astype(jnp.bfloat16)


def per_device(
    hidden,
    lengths,
    attn_gain,
    w_query,
    w_latent,
    latent_gain,
    w_rope_key,
    w_key_up,
    w_value_up,
    w_out,
    latent_cache,
    rope_cache,
    ffn_gain,
    expert_ids,
    route_weights,
    w_gate_up,
    w_down,
):
    row_count = hidden.shape[0]
    head_local = w_key_up.shape[0]
    nope_width = w_key_up.shape[2]
    rope_width = w_rope_key.shape[0]
    score_scale = (nope_width + rope_width) ** (-0.5)
    normed = rms_norm(hidden.astype(jnp.float32), attn_gain).astype(jnp.bfloat16)
    queries = jnp.dot(normed, w_query, preferred_element_type=jnp.float32).astype(jnp.bfloat16)
    queries = queries.reshape(row_count, head_local, nope_width + rope_width)
    query_rope = rotary(queries[:, :, nope_width:].astype(jnp.float32), lengths).astype(
        jnp.bfloat16
    )
    query_latent = jnp.einsum(
        "rhn,hln->rhl", queries[:, :, :nope_width], w_key_up, preferred_element_type=jnp.float32
    ).astype(jnp.bfloat16)
    latent_new = rms_norm(
        jnp.dot(normed, w_latent, preferred_element_type=jnp.float32), latent_gain
    ).astype(jnp.bfloat16)
    key_raw = lax.dot_general(
        normed, w_rope_key, (((1,), (1,)), ((), ())), preferred_element_type=jnp.float32
    )
    key_new = rotary(key_raw, lengths).astype(jnp.bfloat16)
    mixed_latent = attend(
        query_latent,
        query_rope,
        latent_new,
        key_new,
        latent_cache,
        rope_cache,
        lengths,
        score_scale,
    )
    head_out = jnp.einsum(
        "rhl,hlv->rhv", mixed_latent, w_value_up, preferred_element_type=jnp.float32
    ).astype(jnp.bfloat16)
    heads_flat = head_out.reshape(row_count, -1)
    part = jnp.dot(heads_flat, w_out, preferred_element_type=jnp.float32)
    return expert_layer(part, hidden, ffn_gain, expert_ids, route_weights, w_gate_up, w_down)


def solution(mesh):
    in_specs = (
        P("dev", None),
        P("dev"),
        P(),
        P(None, "section"),
        P(),
        P(),
        P(),
        P("section", None, None),
        P("section", None, None),
        P("section", None),
        P("dev", None, None),
        P("dev", None, None),
        P(),
        P("dev", None),
        P("dev", None),
        P("dev", None, "section", None),
        P("dev", "section", None),
    )
    out_specs = P("dev", None)
    return jax.shard_map(
        per_device, mesh=mesh, in_specs=in_specs, out_specs=out_specs, check_vma=False
    )
```

time: 97.1 us -> 77.2 us (0.80)
  Pallas kernels: 66.1 us -> 52.2 us
  matrix products: 20.8 us -> 18.7 us
  other arithmetic: 4.33 us -> 2.65 us
  local copies, waits for them, and re-layouts: 4.68 us -> 3.25 us
    pallas_call x1, Pallas kernels: 66.1 us -> 52.2 us  [expert_layer(): pl.pallas_call(functools.partial(expert_kernel, sections, devices), out_s...]
    dynamic_slice x3 -> x0, local copies, waits for them, and re-layouts: 2.91 us -> none  [the longest x1 1.38 us: per_device(): own_hidden = lax.dynamic_slice_in_dim(hidden, first_row, quarter, 0)]
    dot_general x1, matrix products: 2.74 us -> 1.13 us  [per_device(): part = jnp.dot(heads_flat, w_out, preferred_element_type=jnp.float32)]
    dot_general x1, matrix products: 2.22 us -> 0.61 us  [per_device(): jnp.dot(normed, w_latent, preferred_element_type=jnp.float32)]
    unnamed x13 -> x23, local copies, waits for them, and re-layouts: 1.6 us -> 3.02 us
    dot_general x1, matrix products: 1.54 us -> 0.31 us  [attend(): jnp.einsum('rhp,rpt->rht', query_rope, rope_cache, preferred_element_type...]
    dot_general x1, matrix products: 0.21 us -> 1.32 us  [per_device(): jnp.einsum('rhl,hlv->rhv', mixed_latent, w_value_up, preferred_element_ty...]
    dot_general x1, matrix products: 1.6 us -> 2.67 us  [per_device(): jnp.dot(normed, w_query, preferred_element_type=jnp.float32)]
where the time goes in v1:
time: 77.2 us; the launch traced here: 77 us
  Pallas kernels  52.2 us (68%)
  matrix products  18.7 us (24%)
  local copies, waits for them, and re-layouts  3.25 us (4%)
  other arithmetic  2.65 us (3%)
    pallas_call x1, Pallas kernels, expert_layer(): pl.pallas_call(functools.partial(expert_kernel, sections, devices), out_s...  52.2 us
    dot_general x1, matrix products, attend(): jnp.einsum('rhl,rtl->rht', query_latent, latent_cache, preferred_element_...  5.88 us
    dot_general x1, matrix products, attend(): jnp.einsum('rht,rtl->rhl', prob_cache, latent_cache, preferred_element_ty...  4.76 us
    unnamed x23, local copies, waits for them, and re-layouts  3.02 us
    dot_general x1, matrix products, per_device(): jnp.dot(normed, w_query, preferred_element_type=jnp.float32)  2.67 us

profile of v1, /device:TPU:0, one launch (start us, length us, event | category | flops | bytes accessed | tf_op | source)
XLA Modules:
  0.0 77.0 jit_solution(16100240381610570038)
XLA Ops:
  0.0 1.2 %fusion.5 = f32[32]{0:T(128)S(1)} fusion(bf16[32,2048]{1,0:T(8,128)(2,1)} %param.17), kind=kLoop, calls=%fused_computation.12 | loop fusion | flops 196576 | bytes 131200 | tf_op jit(solution)/shard_map/reduce_sum | solution.py:20
  1.2 1.3 %fusion.34 = f32[32,64]{1,0:T(8,128)S(1)} fusion(bf16[64,2048]{1,0:T(8,128)(2,1)} %param.23, bf16[32,2048]{1,0:T(8,128)(2,1)} %param.17, f32[2048]{0:T(1024)} %param.19, f32[32]{0:T(128)S(1)} %add_rsqrt_fusion.1), kind=kOutput, calls=%fused_computation.61 | convolution fusion | flops 8650752 | bytes 409728 | tf_op jit(solution)/shard_map/dot_general | solution.py:558
  2.5 0.0 copy-start.9
  2.5 0.7 convert_element_type.57
  3.2 0.1 subtract_convert_fusion.1
  3.4 2.7 %convolution_convert_fusion.2 = bf16[32,768]{1,0:T(8,128)(2,1)S(1)} fusion(bf16[2048,768]{1,0:T(8,128)(2,1)} %param.20, bf16[32,2048]{1,0:T(8,128)(2,1)} %param.17, f32[2048]{0:T(1024)} %param.19, f32[32]{0:T(128)S(1)} %add_rsqrt_fusion.1), kind=kOutput, calls=%fused_computation.7 | convolution fusion | flops 100950016 | bytes 3334272 | tf_op jit(solution)/shard_map/dot_general | solution.py:547
  6.1 0.1 reshape.119
  6.2 0.1 subtract_convert_fusion
  6.3 0.1 maximum_bitcast_fusion
  6.4 0.2 fusion.25
  6.6 0.0 copy-done
  6.6 0.3 fusion.31
  7.0 0.3 fusion.1
  7.2 0.0 copy-done.9
  7.3 0.1 iota_compare_fusion
  7.4 0.0 copy-start.5
  7.4 0.0 copy-start.8
  7.4 5.9 %fusion.39 = (f32[32,4]{1,0:T(8,128)S(1)}, f32[32,4,256]{2,1,0:T(4,128)S(1)}) fusion(f32[32,4,256]{2,1,0:T(4,128)S(1)} %fusion.31, bf16[32,256,512]{2,1,0:T(8,128)(2,1)} %param.27, bf16[32,4,512]{2,0,1:T(8,128)(2,1)S(1)} %fusion.1, pred[32,256]{1,0:T(8,128)(4,1)S(1)} %iota_compare_fusion), kind=kOutput, calls=%fused_computation.63 | convolution fusion | flops 33685376 | bytes 8790528 | tf_op jit(solution)/shard_map/rhl,rtl->rht/dot_general | solution.py:491
  13.3 0.0 copy-done.5
  13.3 0.6 multiply_reduce_fusion
  13.9 0.1 fusion.32
  14.0 0.2 fusion.12
  14.3 0.2 fusion.15
  14.5 0.0 copy-start.3
  14.5 4.8 %fusion.16 = f32[32,4,512]{2,1,0:T(4,128)S(1)} fusion(bf16[32,256,512]{2,1,0:T(8,128)(2,1)} %param.27, f32[32,4,256]{2,1,0:T(4,128)S(1)} %get-tuple-element.16, f32[32,4]{1,0:T(8,128)S(1)} %get-tuple-element.10, f32[32,4]{1,0:T(8,128)S(1)} %fusion.28, pred[32,256]{1,0:T(8,128)(4,1)S(1)} %iota_compare_fusion), kind=kOutput, calls=%fused_computation.25 | convolution fusion | flops 33685504 | bytes 8791040 | tf_op jit(solution)/shard_map/rht,rtl->rhl/dot_general | solution.py:514
  19.3 0.1 copy.25
  19.4 1.3 %fusion.4 = bf16[4,4,8,128]{3,2,1,0:T(8,128)(2,1)S(1)} fusion(bf16[4,512,128]{2,1,0:T(8,128)(2,1)} %param.25, f32[32,4,512]{2,1,0:T(4,128)S(1)} %fusion.16, f32[32,512]{1,0:T(8,128)S(1)} %get-tuple-element.7, f32[32,4]{0,1:T(4,128)S(1)} %copy.25), kind=kOutput, calls=%fused_computation.9 | convolution fusion | flops 16990208 | bytes 885248 | tf_op jit(solution)/shard_map/rhl,hlv->rhv/dot_general | solution.py:572
  20.7 1.1 %fusion.part_ref = bf16[4,8,2048]{2,1,0:T(8,128)(2,1)} fusion(bf16[512,2048]{1,0:T(8,128)(2,1)S(1)} %copy-done.3, bf16[4,4,8,128]{3,2,1,0:T(8,128)(2,1)S(1)} %fusion.4), kind=kOutput, calls=%fused_computation.1 | convolution fusion | flops 67174400 | bytes 2260992 | tf_op jit(solution)/shard_map/dot_general | solution.py:576
  21.9 0.7 copy.27
  22.5 0.7 copy.28
  23.2 52.2 %shard_map.163 = bf16[4,8,2048]{2,1,0:T(8,128)(2,1)} custom-call(bf16[4,8,2048]{2,1,0:T(8,128)(2,1)} %fusion.part_ref, bf16[4,8,2048]{2,1,0:T(8,128)(2,1)} %bitcast.32, f32[1,2048]{1,0:T(1,128)} %bitcast.40, s32[4,8,6]{2,1,0:T(8,128)} %bitcast.34, f32[4,8,6]{2,1,0:T(8,128)} %bitcast.35, bf16[8,2,352,2048]{3,2,1,0:T(8,128)(2,1)} %w_up_ref.1, ...), custom_call_target="tpu_custom_call" | custom-call | tf_op jit(solution)/shard_map/pallas_call | solution.py:425
  75.4 1.6 %copy.57 = bf16[32,2048]{1,0:T(8,128)(2,1)} copy(bf16[32,2048]{1,0:T(8,128)(2,1)} %bitcast.33) | data formatting | bytes 262144
  (20 shorter events, 0.1 us)
Async XLA Ops:
  0.0 6.6 %copy-start = (bf16[32,64,256]{2,1,0:T(8,128)(2,1)S(1)}, bf16[32,64,256]{2,1,0:T(8,128)(2,1)}, u32[]{:S(2)}) copy-start(bf16[32,64,256]{2,1,0:T(8,128)(2,1)} %param.28) | copy-start | bytes 3145732
  0.0 7.0 %copy-start.4 = (bf16[4,512,128]{2,1,0:T(8,128)(2,1)S(1)}, bf16[4,512,128]{2,1,0:T(8,128)(2,1)}, u32[]{:S(2)}) copy-start(bf16[4,512,128]{2,1,0:T(8,128)(2,1)} %param.24) | copy-start | bytes 1572868
  2.5 4.8 %copy-start.9 = (s32[32]{0:T(128)S(1)}, s32[32]{0:T(128)}, u32[]{:S(2)}) copy-start(s32[32]{0:T(128)} %param.18) | copy-start | bytes 388
  7.3 5.9 %copy-start.1 = (bf16[32,2048]{1,0:T(8,128)(2,1)S(1)}, bf16[32,2048]{1,0:T(8,128)(2,1)}, u32[]{:S(2)}) copy-start(bf16[32,2048]{1,0:T(8,128)(2,1)} %param.17) | copy-start | bytes 393220
  7.3 5.9 %copy-start.2 = (bf16[2048,512]{1,0:T(8,128)(2,1)S(1)}, bf16[2048,512]{1,0:T(8,128)(2,1)}, u32[]{:S(2)}) copy-start(bf16[2048,512]{1,0:T(8,128)(2,1)} %param.21) | copy-start | bytes 6291460
  7.4 5.9 %copy-start.5 = (f32[2048]{0:T(1024)S(1)}, f32[2048]{0:T(1024)}, u32[]{:S(2)}) copy-start(f32[2048]{0:T(1024)} %param.19) | copy-start | bytes 24580
  7.4 6.5 %copy-start.8 = (f32[512]{0:T(512)S(1)}, f32[512]{0:T(512)}, u32[]{:S(2)}) copy-start(f32[512]{0:T(512)} %param.22) | copy-start | bytes 6148
  14.5 6.2 %copy-start.3 = (bf16[512,2048]{1,0:T(8,128)(2,1)S(1)}, bf16[512,2048]{1,0:T(8,128)(2,1)}, u32[]{:S(2)}) copy-start(bf16[512,2048]{1,0:T(8,128)(2,1)} %param.26) | copy-start | bytes 6291460
  19.3 2.6 %copy-start.6 = (s32[32,6]{0,1:T(8,128)S(1)}, s32[32,6]{0,1:T(8,128)}, u32[]{:S(2)}) copy-start(s32[32,6]{0,1:T(8,128)} %param.30) | copy-start | bytes 2308
  19.3 3.3 %copy-start.7 = (f32[32,6]{0,1:T(8,128)S(1)}, f32[32,6]{0,1:T(8,128)}, u32[]{:S(2)}) copy-start(f32[32,6]{0,1:T(8,128)} %param.31) | copy-start | bytes 2308

commit v2 on v1

--- a/solution.py
+++ b/solution.py
@@ -9,6 +9,7 @@
 
 MOST = 2
 CHUNKS = 4
+CACHE_GROUPS = 8
 MESH = pl.DeviceIdType.MESH
 
 
@@ -21,33 +22,32 @@
     return values * lax.rsqrt(mean_square + epsilon) * norm_gain
 
 
-def rotary(values, positions):
-    half_width = values.shape[-1] // 2
-    step_index = jnp.arange(half_width, dtype=jnp.float32)
-    frequency = jnp.exp(-jnp.log(10000.0) * step_index / half_width)
-    angles = positions.astype(jnp.float32)[:, None] * frequency[None, :]
-    if values.ndim == 3:
-        angles = angles[:, None, :]
-    cosine = jnp.cos(angles)
-    sine_part = jnp.sin(angles)
-    first_half = values[..., :half_width]
-    second = values[..., half_width:]
-    return jnp.concatenate(
-        [first_half * cosine - second * sine_part, second * cosine + first_half * sine_part],
-        axis=-1,
-    )
-
-
-def route_rows(table_ref, ids, weights, experts, place):
-    rows, top = ids.shape
+def turn_of(positions, width):
+    half = width // 2
+    step = lax.broadcasted_iota(jnp.int32, (1, width), 1)
+    step = jnp.where(step < half, step, step - half).astype(jnp.float32)
+    frequency = jnp.exp(-jnp.log(10000.0) * step / half)
+    angles = positions.astype(jnp.float32) * frequency
+    return jnp.cos(angles), jnp.sin(angles)
+
+
+def rotary(values, cosine, sine):
+    half = values.shape[-1] // 2
+    turned = jnp.concatenate([-values[:, half:], values[:, :half]], axis=1)
+    return values * cosine + turned * sine
+
+
+def route_rows(table_ref, ids_ref, weights_ref, first_row, experts, place):
+    rows = table_ref.shape[0]
     lane = lax.broadcasted_iota(jnp.int32, (rows, experts), 1)
     row = lax.broadcasted_iota(jnp.int32, (rows, experts), 0)
     dense = jnp.zeros((rows, experts), jnp.float32)
     routed = jnp.zeros((rows, experts), jnp.float32)
-    for k in range(top):
-        hit = lane == ids[:, k : k + 1]
-        dense = dense + jnp.where(hit, weights[:, k : k + 1], 0.0)
-        routed = routed + jnp.where(hit, 1.0, 0.0)
+    for i in range(rows):
+        for k in range(ids_ref.shape[0]):
+            hit = (row == i) & (lane == ids_ref[k, first_row + i])
+            dense = jnp.where(hit, weights_ref[k, first_row + i], dense)
+            routed = jnp.where(hit, 1.0, routed)
     rank = jnp.zeros((rows, experts), jnp.float32)
     for j in range(rows - 1):
         rank = rank + jnp.where(row > j, routed[j : j + 1, :], 0.0)
@@ -56,17 +56,46 @@
     table_ref[:, experts:] = jnp.where(routed > 0.0, first + rank, -1.0)
 
 
-def expert_kernel(
+def layer_kernel(
     sections,
     devices,
-    part_ref,
-    hidden_ref,
-    gain_ref,
+    lengths_ref,
     ids_ref,
     weights_ref,
+    hidden_ref,
+    attn_gain_ref,
+    latent_gain_ref,
+    ffn_gain_ref,
+    w_query_ref,
+    w_latent_ref,
+    w_rope_key_ref,
+    w_key_up_ref,
+    w_value_up_ref,
+    w_out_ref,
+    latent_cache_ref,
+    rope_cache_ref,
     w_up_ref,
     w_down_ref,
     out_ref,
+    hidden_in,
+    attn_gain,
+    latent_gain,
+    ffn_gain,
+    w_query,
+    w_latent,
+    w_rope_key,
+    w_key_up,
+    w_value_up,
+    w_out,
+    latents,
+    ropes,
+    residual,
+    query_latent,
+    query_rope,
+    self_scores,
+    scores,
+    mixed_latent,
+    part_out,
     w_up,
     w_down,
     part_in,
@@ -88,6 +117,8 @@
     line_in,
     own_out,
     finished,
+    early_sem,
+    cache_sem,
     up_sem,
     down_sem,
     part_send,
@@ -140,13 +171,51 @@
     def down_copy(e):
         return pltpu.make_async_copy(w_down_ref.at[e], w_down.at[e], down_sem.at[e])
 
-    @pl.loop(0, local)
-    def _(e):
-        up_copy(e).start()
-
-    @pl.loop(0, local)
-    def _(e):
-        down_copy(e).start()
+    heads, latent, nope = w_key_up.shape
+    row_count, slots_kept, _ = latents.shape
+    rope = w_rope_key.shape[0]
+    padded = scores.shape[0] // row_count
+    groups = cache_sem.shape[0] // 2
+    group = row_count // groups
+    score_scale = (nope + rope) ** (-0.5)
+    flat = (((1,), (1,)), ((), ()))
+
+    def early_copy(source, landing, n):
+        return pltpu.make_async_copy(source, landing, early_sem.at[n])
+
+    query_copy = early_copy(w_query_ref, w_query, 0)
+    key_up_copy = early_copy(w_key_up_ref, w_key_up, 1)
+    latent_copy = early_copy(w_latent_ref, w_latent, 2)
+    rope_key_copy = early_copy(w_rope_key_ref, w_rope_key, 3)
+    value_up_copy = early_copy(w_value_up_ref, w_value_up, 4)
+    out_copy = early_copy(w_out_ref, w_out, 5)
+
+    def cache_copies(g):
+        held = pl.ds(g * group, group)
+        return (
+            pltpu.make_async_copy(latent_cache_ref.at[held], latents.at[held], cache_sem.at[2 * g]),
+            pltpu.make_async_copy(rope_cache_ref.at[held], ropes.at[held], cache_sem.at[2 * g + 1]),
+        )
+
+    hidden_copy = early_copy(hidden_ref, hidden_in, 6)
+    gain_copies = (
+        early_copy(attn_gain_ref, attn_gain, 7),
+        early_copy(latent_gain_ref, latent_gain, 8),
+        early_copy(ffn_gain_ref, ffn_gain, 9),
+    )
+
+    hidden_copy.start()
+    for copy in gain_copies:
+        copy.start()
+    query_copy.start()
+    key_up_copy.start()
+    latent_copy.start()
+    rope_key_copy.start()
+    for g in range(groups):
+        for copy in cache_copies(g):
+            copy.start()
+    value_up_copy.start()
+    out_copy.start()
 
     barrier = pltpu.get_barrier_semaphore()
 
@@ -157,11 +226,96 @@
             barrier, inc=1, device_id=(lax.rem(t, sections), t // sections), device_id_type=MESH
         )
 
+    row = lax.broadcasted_iota(jnp.int32, (row_count, rope), 0)
+    positions = jnp.zeros((row_count, rope), jnp.int32)
+    for r in range(row_count):
+        positions = jnp.where(row == r, lengths_ref[r], positions)
+    cosine, sine = turn_of(positions, rope)
+    hidden_copy.wait()
+    for copy in gain_copies:
+        copy.wait()
+    hidden = hidden_in[...].astype(f32)
+    residual[...] = hidden
+    normed = rms_norm(hidden, attn_gain[...]).astype(bf16)
+    query_latent[...] = jnp.zeros_like(query_latent)
+    query_rope[...] = jnp.zeros_like(query_rope)
+    query_copy.wait()
+    queries = jnp.dot(normed, w_query[...], preferred_element_type=f32).astype(bf16).astype(f32)
+    rope_key_copy.wait()
+    latent_copy.wait()
+    key_raw = lax.dot_general(normed, w_rope_key[...], flat, preferred_element_type=f32)
+    key_new = rotary(key_raw, cosine, sine).astype(bf16).astype(f32)
+    latent_raw = jnp.dot(normed, w_latent[...], preferred_element_type=f32)
+    latent_new = rms_norm(latent_raw, latent_gain[...]).astype(bf16).astype(f32)
+    key_up_copy.wait()
+    for h in range(heads):
+        first = h * (nope + rope)
+        turned = rotary(queries[:, first + nope : first + nope + rope], cosine, sine)
+        turned = turned.astype(bf16).astype(f32)
+        mapped = lax.dot_general(
+            queries[:, first : first + nope].astype(bf16),
+            w_key_up[h],
+            flat,
+            preferred_element_type=f32,
+        )
+        mapped = mapped.astype(bf16).astype(f32)
+        query_latent[:, h, :] = mapped
+        query_rope[:, h, :] = turned
+        own_score = jnp.sum(mapped * latent_new, axis=1, keepdims=True) + jnp.sum(
+            turned * key_new, axis=1, keepdims=True
+        )
+        self_scores[:, h, :] = jnp.broadcast_to(own_score * score_scale, (row_count, 128))
+
+    place = lax.broadcasted_iota(jnp.int32, (padded, slots_kept), 1)
+    for g in range(groups):
+        for copy in cache_copies(g):
+            copy.wait()
+        for e in range(g * local // groups, (g + 1) * local // groups):
+            up_copy(e).start()
+        for r in range(g * group, (g + 1) * group):
+            found = lax.dot_general(
+                query_latent[r].astype(bf16), latents[r], flat, preferred_element_type=f32
+            ) + jnp.dot(query_rope[r].astype(bf16), ropes[r], preferred_element_type=f32)
+            scores[r * padded : (r + 1) * padded, :] = jnp.where(
+                place < lengths_ref[r], found * score_scale, far_below
+            )
+    for e in range(local):
+        down_copy(e).start()
+
+    own_scores = self_scores[...].reshape(row_count * padded, 128)[:, :1]
+    peak = jnp.maximum(jnp.max(scores[...], axis=1, keepdims=True), own_scores)
+    likely = jnp.exp(scores[...] - peak)
+    own_likely = jnp.exp(own_scores - peak)
+    totals = jnp.sum(likely, axis=1, keepdims=True) + own_likely
+    scores[...] = likely / totals
+    own_probs = (own_likely / totals).astype(bf16).astype(f32)
+    self_scores[...] = jnp.broadcast_to(own_probs, (row_count * padded, 128)).reshape(
+        row_count, padded, 128
+    )
+
+    for r in range(row_count):
+        mixed_latent[r] = jnp.dot(
+            scores[r * padded : (r + 1) * padded, :].astype(bf16),
+            latents[r],
+            preferred_element_type=f32,
+        )
+    value_up_copy.wait()
+    head_outs = []
+    for h in range(heads):
+        mixed = mixed_latent[:, h, :] + self_scores[:, h, :1] * latent_new
+        head_outs.append(
+            jnp.dot(mixed.astype(bf16), w_value_up[h], preferred_element_type=f32).astype(bf16)
+        )
+    out_copy.wait()
+    part = jnp.dot(jnp.concatenate(head_outs, axis=1), w_out[...], preferred_element_type=f32)
+    for t in range(sections):
+        part_out[t] = part[t * quarter : (t + 1) * quarter, :].astype(bf16)
+
     pl.semaphore_wait(barrier, total - 1)
 
     def part_copy(i, here):
         t = lax.rem(section + i, sections)
-        return remote(part_ref.at[t], part_in.at[here], part_send.at[i], part_recv.at[here], (t, dev))
+        return remote(part_out.at[t], part_in.at[here], part_send.at[i], part_recv.at[here], (t, dev))
 
     for i in range(1, sections):
         part_copy(i, section).start()
@@ -172,7 +326,7 @@
         )
 
     here = place_of(me)
-    route_rows(table, ids_ref[section], weights_ref[section], experts, here)
+    route_rows(table, ids_ref, weights_ref, section * quarter, experts, here)
     tables[here] = table[...]
 
     def table_copy(i, landing):
@@ -189,14 +343,15 @@
     def _(i):
         table_copy(i, here).start()
 
-    summed = hidden_ref[section].astype(f32) + part_ref[section].astype(f32)
+    mine = pl.ds(pl.multiple_of(section * quarter, quarter), quarter)
+    summed = residual[mine, :] + part_out[section].astype(f32)
     for i in range(1, sections):
         t = lax.rem(section + i, sections)
         part_copy(i, t).wait_recv()
         summed = summed + part_in[t].astype(f32)
     middle_rows = summed.astype(bf16).astype(f32)
     middle[...] = middle_rows
-    normed = rms_norm(middle_rows, gain_ref[...]).astype(bf16)
+    normed = rms_norm(middle_rows, ffn_gain[...]).astype(bf16)
 
     def line_copy(k, i, slot):
         t = lax.rem(line + i, pairs)
@@ -263,7 +418,6 @@
             plane_copy(k, i, lax.rem(section + i, sections)).wait_recv()
         pair_copy(k, core).start()
 
-    flat = (((1,), (1,)), ((), ()))
     to_partner(0)
     for k in range(chunks):
         if k + 1 < chunks:
@@ -405,29 +559,71 @@
         back_pair_copy(k, 1 - core).wait_send()
 
 
-def expert_layer(part, hidden, ffn_gain, expert_ids, route_weights, w_gate_up, w_down):
+def per_device(
+    hidden,
+    lengths,
+    attn_gain,
+    w_query,
+    w_latent,
+    latent_gain,
+    w_rope_key,
+    w_key_up,
+    w_value_up,
+    w_out,
+    latent_cache,
+    rope_cache,
+    ffn_gain,
+    expert_ids,
+    route_weights,
+    w_gate_up,
+    w_down,
+):
     sections = lax.axis_size("section")
     devices = lax.axis_size("dev")
     total = sections * devices
     pairs = devices // 2
     row_count, width = hidden.shape
     quarter = row_count // sections
+    heads, latent, _ = w_key_up.shape
+    rope, slots_kept = rope_cache.shape[1:]
     local, _, units, _ = w_gate_up.shape
     experts = local * devices
     slots = total * MOST
     rows = total * quarter
     chunks = CHUNKS
     span = width // chunks
+    groups = CACHE_GROUPS
+    padded = -(-heads // 8) * 8
     bf16, f32 = jnp.bfloat16, jnp.float32
     vmem = pl.BlockSpec(memory_space=pltpu.VMEM)
+    smem = pl.BlockSpec(memory_space=pltpu.SMEM)
     anywhere = pl.BlockSpec(memory_space=pl.ANY)
     sems = lambda *count: pltpu.SemaphoreType.DMA(count)
     out = pl.pallas_call(
-        functools.partial(expert_kernel, sections, devices),
+        functools.partial(layer_kernel, sections, devices),
         out_shape=jax.ShapeDtypeStruct((sections, quarter, width), bf16),
-        in_specs=[vmem] * 5 + [anywhere] * 2,
+        in_specs=[smem] * 3 + [anywhere] * 14,
         out_specs=vmem,
         scratch_shapes=[
+            pltpu.VMEM(hidden.shape, bf16),
+            pltpu.VMEM((1, width), f32),
+            pltpu.VMEM((1, latent), f32),
+            pltpu.VMEM((1, width), f32),
+            pltpu.VMEM(w_query.shape, bf16),
+            pltpu.VMEM(w_latent.shape, bf16),
+            pltpu.VMEM(w_rope_key.shape, bf16),
+            pltpu.VMEM(w_key_up.shape, bf16),
+            pltpu.VMEM(w_value_up.shape, bf16),
+            pltpu.VMEM(w_out.shape, bf16),
+            pltpu.VMEM(latent_cache.shape, bf16),
+            pltpu.VMEM(rope_cache.shape, bf16),
+            pltpu.VMEM((row_count, width), f32),
+            pltpu.VMEM((row_count, padded, latent), f32),
+            pltpu.VMEM((row_count, padded, rope), f32),
+            pltpu.VMEM((row_count, padded, 128), f32),
+            pltpu.VMEM((row_count * padded, slots_kept), f32),
+            pltpu.VMEM((row_count, padded, latent), f32),
+            pltpu.VMEM((sections, quarter, width), bf16),
             pltpu.VMEM(w_gate_up.shape, bf16),
             pltpu.VMEM(w_down.shape, bf16),
             pltpu.VMEM((sections, quarter, width), bf16),
@@ -449,6 +645,8 @@
             pltpu.VMEM((chunks, pairs, quarter, span), bf16),
             pltpu.VMEM((chunks, quarter, span), bf16),
             pltpu.VMEM((chunks, sections, quarter, span), bf16),
+            sems(10),
+            sems(2 * groups),
             sems(local),
             sems(local),
             sems(sections),
@@ -471,110 +669,28 @@
             sems(chunks, sections),
         ],
         compiler_params=pltpu.CompilerParams(
-            collective_id=0, has_side_effects=True, vmem_limit_bytes=62 * 1024 * 1024
+            collective_id=0, has_side_effects=True, vmem_limit_bytes=63 * 1024 * 1024
         ),
     )(
-        part.astype(bf16).reshape(sections, quarter, width),
-        hidden.reshape(sections, quarter, width),
+        lengths,
+        expert_ids.T,
+        route_weights.T,
+        hidden,
+        attn_gain.reshape(1, width),
+        latent_gain.reshape(1, latent),
         ffn_gain.reshape(1, width),
-        expert_ids.reshape(sections, quarter, -1),
-        route_weights.reshape(sections, quarter, -1),
+        w_query,
+        w_latent,
+        w_rope_key,
+        w_key_up,
+        w_value_up,
+        w_out,
+        latent_cache,
+        rope_cache,
         w_gate_up,
         w_down,
     )
     return out.reshape(row_count, width)
-
-
-def attend(
-    query_latent, query_rope, latent_new, key_new, latent_cache, rope_cache, lengths, score_scale
-):
-    scores = jnp.einsum(
-        "rhl,rtl->rht", query_latent, latent_cache, preferred_element_type=jnp.float32
-    )
-    scores = scores + jnp.einsum(
-        "rhp,rpt->rht", query_rope, rope_cache, preferred_element_type=jnp.float32
-    )
-    scores = scores * score_scale
-    self_score = jnp.einsum(
-        "rhl,rl->rh", query_latent, latent_new, preferred_element_type=jnp.float32
-    )
-    self_score = (
-        self_score
-        + jnp.einsum("rhp,rp->rh", query_rope, key_new, preferred_element_type=jnp.float32)
-    ) * score_scale
-    places = jnp.arange(latent_cache.shape[1], dtype=jnp.int32)
-    valid_mask = places[None, None, :] < lengths[:, None, None]
-    masked = jnp.where(valid_mask, scores, far_below)
-    peak_score = jnp.maximum(jnp.max(masked, axis=2), self_score)
-    weights = jnp.where(valid_mask, jnp.exp(masked - peak_score[:, :, None]), 0.0)
-    self_weight = jnp.exp(self_score - peak_score)
-    totals = jnp.sum(weights, axis=2) + self_weight
-    prob_cache = (weights / totals[:, :, None]).astype(jnp.bfloat16)
-    prob_self = (self_weight / totals).astype(jnp.bfloat16)
-    mixed = jnp.einsum("rht,rtl->rhl", prob_cache, latent_cache, preferred_element_type=jnp.float32)
-    mixed = (
-        mixed
-        + prob_self.astype(jnp.float32)[:, :, None] * latent_new.astype(jnp.float32)[:, None, :]
-    )
-    return mixed.astype(jnp.bfloat16)
-
-
-def per_device(
-    hidden,
-    lengths,
-    attn_gain,
-    w_query,
-    w_latent,
-    latent_gain,
-    w_rope_key,
-    w_key_up,
-    w_value_up,
-    w_out,
-    latent_cache,
-    rope_cache,
-    ffn_gain,
-    expert_ids,
-    route_weights,
-    w_gate_up,
-    w_down,
-):
-    row_count = hidden.shape[0]
-    head_local = w_key_up.shape[0]
-    nope_width = w_key_up.shape[2]
-    rope_width = w_rope_key.shape[0]
-    score_scale = (nope_width + rope_width) ** (-0.5)
-    normed = rms_norm(hidden.astype(jnp.float32), attn_gain).astype(jnp.bfloat16)
-    queries = jnp.dot(normed, w_query, preferred_element_type=jnp.float32).astype(jnp.bfloat16)
-    queries = queries.reshape(row_count, head_local, nope_width + rope_width)
-    query_rope = rotary(queries[:, :, nope_width:].astype(jnp.float32), lengths).astype(
-        jnp.bfloat16
-    )
-    query_latent = jnp.einsum(
-        "rhn,hln->rhl", queries[:, :, :nope_width], w_key_up, preferred_element_type=jnp.float32
-    ).astype(jnp.bfloat16)
-    latent_new = rms_norm(
-        jnp.dot(normed, w_latent, preferred_element_type=jnp.float32), latent_gain
-    ).astype(jnp.bfloat16)
-    key_raw = lax.dot_general(
-        normed, w_rope_key, (((1,), (1,)), ((), ())), preferred_element_type=jnp.float32
-    )
-    key_new = rotary(key_raw, lengths).astype(jnp.bfloat16)
-    mixed_latent = attend(
-        query_latent,
-        query_rope,
-        latent_new,
-        key_new,
-        latent_cache,
-        rope_cache,
-        lengths,
-        score_scale,
-    )
-    head_out = jnp.einsum(
-        "rhl,hlv->rhv", mixed_latent, w_value_up, preferred_element_type=jnp.float32
-    ).astype(jnp.bfloat16)
-    heads_flat = head_out.reshape(row_count, -1)
-    part = jnp.dot(heads_flat, w_out, preferred_element_type=jnp.float32)
-    return expert_layer(part, hidden, ffn_gain, expert_ids, route_weights, w_gate_up, w_down)
 
 
 def solution(mesh):

time: 77.2 us -> 61.2 us (0.79)
  matrix products: 18.7 us -> 0 us
  Pallas kernels: 52.2 us -> 59.5 us
  other arithmetic: 2.65 us -> 0 us
  local copies, waits for them, and re-layouts: 3.25 us -> 1.57 us
    dot_general x11 -> x0, matrix products: 18.7 us -> none  [the longest x1 5.88 us: attend(): jnp.einsum('rhl,rtl->rht', query_latent, latent_cache, preferred_element_...]
    pallas_call x1, Pallas kernels: 52.2 us -> 59.5 us  [per_device(): pl.pallas_call(functools.partial(layer_kernel, sections, devices), out_sh...]
    unnamed x23 -> x1, local copies, waits for them, and re-layouts: 3.02 us -> 1.57 us
    reduce_sum x2 -> x0, other arithmetic: 1.38 us -> none  [the longest x1 1.15 us: rms_norm(): mean_square = jnp.mean(values * values, axis=-1, keepdims=True)]
    convert_element_type x4 -> x0, other arithmetic: 0.84 us -> none  [the longest x1 0.73 us: rotary(): angles = positions.astype(jnp.float32)[:, None] * frequency[None, :]]
where the time goes in v2:
time: 61.2 us; the launch traced here: 61 us
  Pallas kernels  59.5 us (97%)
  local copies, waits for them, and re-layouts  1.57 us (3%)
    pallas_call x1, Pallas kernels, per_device(): pl.pallas_call(functools.partial(layer_kernel, sections, devices), out_sh...  59.5 us
    unnamed x1, local copies, waits for them, and re-layouts  1.57 us

profile of v2, /device:TPU:0, one launch (start us, length us, event | category | flops | bytes accessed | tf_op | source)
XLA Modules:
  0.0 61.0 jit_solution(12420084446867852826)
XLA Ops:
  0.0 59.5 %shard_map.163 = bf16[4,8,2048]{2,1,0:T(8,128)(2,1)} custom-call(s32[32]{0:T(128)} %lengths_ref.1, s32[6,32]{1,0:T(8,128)} %bitcast.9, f32[6,32]{1,0:T(8,128)} %bitcast.10, bf16[32,2048]{1,0:T(8,128)(2,1)} %hidden_ref.1, f32[1,2048]{1,0:T(1,128)} %bitcast.7, f32[1,512]{1,0:T(1,128)} %bitcast.11, f32[1,2048]{1,0:T(1,128)} %bitcast.8, ...), custom_call_target="tpu_custom_call" | custom-call | tf_op jit(solution)/shard_map/pallas_call | solution.py:602
  59.5 1.6 %copy.19 = bf16[32,2048]{1,0:T(8,128)(2,1)} copy(bf16[32,2048]{1,0:T(8,128)(2,1)} %bitcast.6) | data formatting | bytes 262144

commit v3 on v2

--- a/solution.py
+++ b/solution.py
@@ -8,8 +8,9 @@
 from jax.sharding import PartitionSpec as P
 
 MOST = 2
-CHUNKS = 4
-CACHE_GROUPS = 8
+OUT_CHUNKS = 4
+BACK_CHUNKS = 4
+CACHE_GROUPS = 4
 MESH = pl.DeviceIdType.MESH
 
 
@@ -59,9 +60,9 @@
 def layer_kernel(
     sections,
     devices,
-    lengths_ref,
-    ids_ref,
-    weights_ref,
+    lengths_in,
+    ids_in,
+    weights_in,
     hidden_ref,
     attn_gain_ref,
     latent_gain_ref,
@@ -77,6 +78,9 @@
     w_up_ref,
     w_down_ref,
     out_ref,
+    lengths_ref,
+    ids_ref,
+    weights_ref,
     hidden_in,
     attn_gain,
     latent_gain,
@@ -139,6 +143,7 @@
     back_line_recv,
     done_send,
     done_recv,
+    finish_sem,
 ):
     section = lax.axis_index("section")
     dev = lax.axis_index("dev")
@@ -148,7 +153,8 @@
     total = sections * devices
     me = dev * sections + section
     local, _, units, width = w_up.shape
-    chunks, quarter, span = own.shape
+    out_chunks, quarter, out_span = own.shape
+    chunks, span = pair_sum.shape[0], pair_sum.shape[-1]
     rows = total * quarter
     experts = tables.shape[-1] // 2
     slots = packed.shape[0] // local
@@ -198,14 +204,17 @@
         )
 
     hidden_copy = early_copy(hidden_ref, hidden_in, 6)
-    gain_copies = (
+    small_copies = (
         early_copy(attn_gain_ref, attn_gain, 7),
         early_copy(latent_gain_ref, latent_gain, 8),
         early_copy(ffn_gain_ref, ffn_gain, 9),
+        early_copy(lengths_in, lengths_ref, 10),
+        early_copy(ids_in, ids_ref, 11),
+        early_copy(weights_in, weights_ref, 12),
     )
 
     hidden_copy.start()
-    for copy in gain_copies:
+    for copy in small_copies:
         copy.start()
     query_copy.start()
     key_up_copy.start()
@@ -226,19 +235,20 @@
             barrier, inc=1, device_id=(lax.rem(t, sections), t // sections), device_id_type=MESH
         )
 
+    for copy in small_copies:
+        copy.wait()
     row = lax.broadcasted_iota(jnp.int32, (row_count, rope), 0)
     positions = jnp.zeros((row_count, rope), jnp.int32)
     for r in range(row_count):
         positions = jnp.where(row == r, lengths_ref[r], positions)
     cosine, sine = turn_of(positions, rope)
     hidden_copy.wait()
-    for copy in gain_copies:
-        copy.wait()
     hidden = hidden_in[...].astype(f32)
     residual[...] = hidden
     normed = rms_norm(hidden, attn_gain[...]).astype(bf16)
     query_latent[...] = jnp.zeros_like(query_latent)
     query_rope[...] = jnp.zeros_like(query_rope)
+    self_scores[...] = jnp.zeros_like(self_scores)
     query_copy.wait()
     queries = jnp.dot(normed, w_query[...], preferred_element_type=f32).astype(bf16).astype(f32)
     rope_key_copy.wait()
@@ -264,61 +274,11 @@
         own_score = jnp.sum(mapped * latent_new, axis=1, keepdims=True) + jnp.sum(
             turned * key_new, axis=1, keepdims=True
         )
-        self_scores[:, h, :] = jnp.broadcast_to(own_score * score_scale, (row_count, 128))
-
-    place = lax.broadcasted_iota(jnp.int32, (padded, slots_kept), 1)
-    for g in range(groups):
-        for copy in cache_copies(g):
-            copy.wait()
-        for e in range(g * local // groups, (g + 1) * local // groups):
-            up_copy(e).start()
-        for r in range(g * group, (g + 1) * group):
-            found = lax.dot_general(
-                query_latent[r].astype(bf16), latents[r], flat, preferred_element_type=f32
-            ) + jnp.dot(query_rope[r].astype(bf16), ropes[r], preferred_element_type=f32)
-            scores[r * padded : (r + 1) * padded, :] = jnp.where(
-                place < lengths_ref[r], found * score_scale, far_below
-            )
-    for e in range(local):
-        down_copy(e).start()
-
-    own_scores = self_scores[...].reshape(row_count * padded, 128)[:, :1]
-    peak = jnp.maximum(jnp.max(scores[...], axis=1, keepdims=True), own_scores)
-    likely = jnp.exp(scores[...] - peak)
-    own_likely = jnp.exp(own_scores - peak)
-    totals = jnp.sum(likely, axis=1, keepdims=True) + own_likely
-    scores[...] = likely / totals
-    own_probs = (own_likely / totals).astype(bf16).astype(f32)
-    self_scores[...] = jnp.broadcast_to(own_probs, (row_count * padded, 128)).reshape(
-        row_count, padded, 128
-    )
-
-    for r in range(row_count):
-        mixed_latent[r] = jnp.dot(
-            scores[r * padded : (r + 1) * padded, :].astype(bf16),
-            latents[r],
-            preferred_element_type=f32,
-        )
-    value_up_copy.wait()
-    head_outs = []
-    for h in range(heads):
-        mixed = mixed_latent[:, h, :] + self_scores[:, h, :1] * latent_new
-        head_outs.append(
-            jnp.dot(mixed.astype(bf16), w_value_up[h], preferred_element_type=f32).astype(bf16)
-        )
-    out_copy.wait()
-    part = jnp.dot(jnp.concatenate(head_outs, axis=1), w_out[...], preferred_element_type=f32)
-    for t in range(sections):
-        part_out[t] = part[t * quarter : (t + 1) * quarter, :].astype(bf16)
+        self_scores[pl.ds(h, row_count, stride=padded), :] = jnp.broadcast_to(
+            own_score * score_scale, (row_count, 128)
+        )
 
     pl.semaphore_wait(barrier, total - 1)
-
-    def part_copy(i, here):
-        t = lax.rem(section + i, sections)
-        return remote(part_out.at[t], part_in.at[here], part_send.at[i], part_recv.at[here], (t, dev))
-
-    for i in range(1, sections):
-        part_copy(i, section).start()
 
     def place_of(t):
         return (lax.rem(t // sections, 2) * sections + lax.rem(t, sections)) * pairs + t // (
@@ -342,6 +302,65 @@
     @pl.loop(1, total)
     def _(i):
         table_copy(i, here).start()
+
+    position = lax.broadcasted_iota(jnp.int32, (padded, slots_kept), 1)
+
+    def score_rows(g):
+        for r in range(g * group, (g + 1) * group):
+            found = lax.dot_general(
+                query_latent[r].astype(bf16), latents[r], flat, preferred_element_type=f32
+            ) + jnp.dot(query_rope[r].astype(bf16), ropes[r], preferred_element_type=f32)
+            scores[r * padded : (r + 1) * padded, :] = jnp.where(
+                position < lengths_ref[r], found * score_scale, far_below
+            )
+
+    def mix_rows(g):
+        held = slice(g * group * padded, (g + 1) * group * padded)
+        own_scores = self_scores[held, :1]
+        peak = jnp.maximum(jnp.max(scores[held, :], axis=1, keepdims=True), own_scores)
+        likely = jnp.exp(scores[held, :] - peak)
+        own_likely = jnp.exp(own_scores - peak)
+        totals = jnp.sum(likely, axis=1, keepdims=True) + own_likely
+        probs = (likely / totals).astype(bf16)
+        own_probs = (own_likely / totals).astype(bf16).astype(f32)
+        self_scores[held, :] = jnp.broadcast_to(own_probs, (group * padded, 128))
+        for n in range(group):
+            r = g * group + n
+            mixed_latent[r] = jnp.dot(
+                probs[n * padded : (n + 1) * padded, :], latents[r], preferred_element_type=f32
+            )
+
+    for g in range(groups):
+        for copy in cache_copies(g):
+            copy.wait()
+        for e in range(g * local // groups, (g + 1) * local // groups):
+            up_copy(e).start()
+        score_rows(g)
+        if g > 0:
+            mix_rows(g - 1)
+    for e in range(local):
+        down_copy(e).start()
+    mix_rows(groups - 1)
+
+    value_up_copy.wait()
+    head_outs = []
+    for h in range(heads):
+        rows_of = pl.ds(h, row_count, stride=padded)
+        mixed = mixed_latent[:, h, :] + self_scores[rows_of, :][:, :1] * latent_new
+        head_outs.append(
+            jnp.dot(mixed.astype(bf16), w_value_up[h], preferred_element_type=f32).astype(bf16)
+        )
+    out_copy.wait()
+    part = jnp.dot(jnp.concatenate(head_outs, axis=1), w_out[...], preferred_element_type=f32)
+    for t in range(sections):
+        part_out[t] = part[t * quarter : (t + 1) * quarter, :].astype(bf16)
+
+    def part_copy(i, here):
+        t = lax.rem(section + i, sections)
+        return remote(part_out.at[t], part_in.at[here], part_send.at[i], part_recv.at[here], (t, dev))
+
+    for i in range(1, sections):
+        part_copy(i, section).start()
 
     mine = pl.ds(pl.multiple_of(section * quarter, quarter), quarter)
     summed = residual[mine, :] + part_out[section].astype(f32)
@@ -363,12 +382,13 @@
             (section, 2 * t + core),
         )
 
-    def plane_copy(k, i, source):
+    def plane_copy(k, i, source, slot):
+        block = rows_all.at[k, core, source, slot]
         return remote(
-            rows_all.at[k, core, source],
-            rows_all.at[k, core, source],
-            plane_send.at[k, i],
-            plane_recv.at[k, source],
+            block,
+            block,
+            plane_send.at[k, i, slot],
+            plane_recv.at[k, source, slot],
             (lax.rem(section + i, sections), dev),
         )
 
@@ -377,22 +397,25 @@
             rows_all.at[k, which], rows_all.at[k, which], pair_send.at[k], pair_recv.at[k], partner
         )
 
-    for k in range(chunks):
-        own[k] = normed[:, k * span : (k + 1) * span]
-        rows_all[k, core, section, line] = normed[:, k * span : (k + 1) * span]
+    for k in range(out_chunks):
+        own[k] = normed[:, k * out_span : (k + 1) * out_span]
+        rows_all[k, core, section, line] = normed[:, k * out_span : (k + 1) * out_span]
 
         @pl.loop(1, pairs)
         def _(i):
             line_copy(k, i, line).start()
 
-    for k in range(chunks):
+    for k in range(out_chunks):
+        for i in range(1, sections):
+            plane_copy(k, i, section, line).start()
+    for k in range(out_chunks):
 
         @pl.loop(1, pairs)
-        def _(i):
-            line_copy(k, i, lax.rem(line + i, pairs)).wait_recv()
-
-        for i in range(1, sections):
-            plane_copy(k, i, section).start()
+        def _(j):
+            slot = lax.rem(line + j, pairs)
+            line_copy(k, j, slot).wait_recv()
+            for i in range(1, sections):
+                plane_copy(k, i, section, slot).start()
 
     @pl.loop(1, total)
     def _(i):
@@ -414,16 +437,20 @@
     mix[...] = jnp.where(chosen, weight_map, 0.0).astype(bf16)
 
     def to_partner(k):
-        for i in range(1, sections):
-            plane_copy(k, i, lax.rem(section + i, sections)).wait_recv()
+        @pl.loop(0, pairs)
+        def _(j):
+            slot = lax.rem(line + j, pairs)
+            for i in range(1, sections):
+                plane_copy(k, i, lax.rem(section + i, sections), slot).wait_recv()
+
         pair_copy(k, core).start()
 
     to_partner(0)
-    for k in range(chunks):
-        if k + 1 < chunks:
+    for k in range(out_chunks):
+        if k + 1 < out_chunks:
             to_partner(k + 1)
         pair_copy(k, 1 - core).wait_recv()
-        block = rows_all[k].astype(f32).reshape(rows, span).astype(bf16)
+        block = rows_all[k].astype(f32).reshape(rows, out_span).astype(bf16)
         packed[...] = lax.dot_general(
             pick[...], block, (((0,), (0,)), ((), ())), preferred_element_type=f32
         ).astype(bf16)
@@ -433,13 +460,13 @@
             held = slice(e * slots, (e + 1) * slots)
             both = lax.dot_general(
                 packed[held, :],
-                w_up[e, :, :, k * span : (k + 1) * span].reshape(2 * units, span),
+                w_up[e, :, :, k * out_span : (k + 1) * out_span].reshape(2 * units, out_span),
                 flat,
                 preferred_element_type=f32,
             )
             if k > 0:
                 both = both + lifted[held, :]
-            if k + 1 < chunks:
+            if k + 1 < out_chunks:
                 lifted[held, :] = both
             else:
                 gate, lift = both[:, :units], both[:, units:]
@@ -450,13 +477,13 @@
             sum_out.at[k, which], pair_in.at[k], back_pair_send.at[k], back_pair_recv.at[k], partner
         )
 
-    def back_plane_copy(k, i, landing):
+    def back_plane_copy(k, i, landing, slot):
         t = lax.rem(section + i, sections)
         return remote(
-            pair_sum.at[k, t],
-            plane_in.at[k, landing],
-            back_plane_send.at[k, i],
-            back_plane_recv.at[k, landing],
+            pair_sum.at[k, t, slot],
+            plane_in.at[k, landing, slot],
+            back_plane_send.at[k, i, slot],
+            back_plane_recv.at[k, landing, slot],
             (t, dev),
         )
 
@@ -482,29 +509,33 @@
     def over_plane(k):
         back_pair_copy(k, 1 - core).wait_recv()
         pair_sum[k] = (sum_out[k, core].astype(f32) + pair_in[k].astype(f32)).astype(bf16)
-        for i in range(1, sections):
-            back_plane_copy(k, i, section).start()
-
-    def over_line(k):
-        added = pair_sum[k, section].astype(f32)
+
+        @pl.loop(1, pairs)
+        def _(j):
+            for i in range(1, sections):
+                back_plane_copy(k, i, section, lax.rem(line + j, pairs)).start()
+
+    def plane_total(k, slot):
+        added = pair_sum[k, section, slot].astype(f32)
         for i in range(1, sections):
             t = lax.rem(section + i, sections)
-            back_plane_copy(k, i, t).wait_recv()
-            added = added + plane_in[k, t].astype(f32)
-        plane_sum[k] = added.astype(bf16)
-
+            back_plane_copy(k, i, t, slot).wait_recv()
+            added = added + plane_in[k, t, slot].astype(f32)
+        return added
+
+    def over_line(k):
         @pl.loop(1, pairs)
-        def _(i):
-            back_line_copy(k, i, line).start()
-
-        line_in[k, line] = plane_sum[k, line]
+        def _(j):
+            slot = lax.rem(line + j, pairs)
+            plane_sum[k, slot] = plane_total(k, slot).astype(bf16)
+            back_line_copy(k, j, line).start()
 
     def over_sections(k):
-        @pl.loop(1, pairs)
-        def _(i):
-            back_line_copy(k, i, lax.rem(line + i, pairs)).wait_recv()
-
-        result = middle[:, k * span : (k + 1) * span] + jnp.sum(line_in[k].astype(f32), axis=0)
+        result = middle[:, k * span : (k + 1) * span] + plane_total(k, line)
+        for i in range(1, pairs):
+            slot = lax.rem(line + i, pairs)
+            back_line_copy(k, i, slot).wait_recv()
+            result = result + line_in[k, slot].astype(f32)
         own_out[k] = result.astype(bf16)
         finished[k, section] = result.astype(bf16)
         for i in range(1, sections):
@@ -529,13 +560,22 @@
             over_plane(k - 1)
     over_plane(chunks - 1)
     for k in range(chunks):
+        for i in range(1, sections):
+            back_plane_copy(k, i, section, line).start()
+    for k in range(chunks):
         over_line(k)
     for k in range(chunks):
         over_sections(k)
+
+    def finish_copy(k):
+        return pltpu.make_async_copy(
+            finished.at[k], out_ref.at[:, :, pl.ds(k * span, span)], finish_sem.at[k]
+        )
+
     for k in range(chunks):
         for i in range(1, sections):
             done_copy(k, i, lax.rem(section + i, sections)).wait_recv()
-        out_ref[:, :, k * span : (k + 1) * span] = finished[k]
+        finish_copy(k).start()
 
     for i in range(1, sections):
         part_copy(i, section).wait_send()
@@ -544,19 +584,34 @@
     def _(i):
         table_copy(i, here).wait_send()
 
-    for k in range(chunks):
+    for k in range(out_chunks):
 
         @pl.loop(1, pairs)
         def _(i):
             line_copy(k, i, line).wait_send()
+
+        @pl.loop(0, pairs)
+        def _(j):
+            for i in range(1, sections):
+                plane_copy(k, i, section, j).wait_send()
+
+        pair_copy(k, core).wait_send()
+
+    for k in range(chunks):
+
+        @pl.loop(1, pairs)
+        def _(i):
             back_line_copy(k, i, line).wait_send()
 
+        @pl.loop(0, pairs)
+        def _(j):
+            for i in range(1, sections):
+                back_plane_copy(k, i, section, j).wait_send()
+
         for i in range(1, sections):
-            plane_copy(k, i, section).wait_send()
-            back_plane_copy(k, i, section).wait_send()
             done_copy(k, i, section).wait_send()
-        pair_copy(k, core).wait_send()
         back_pair_copy(k, 1 - core).wait_send()
+        finish_copy(k).wait()
 
 
 def per_device(
@@ -590,21 +645,22 @@
     experts = local * devices
     slots = total * MOST
     rows = total * quarter
-    chunks = CHUNKS
-    span = width // chunks
+    out_chunks, chunks = OUT_CHUNKS, BACK_CHUNKS
+    out_span, span = width // out_chunks, width // chunks
     groups = CACHE_GROUPS
     padded = -(-heads // 8) * 8
     bf16, f32 = jnp.bfloat16, jnp.float32
-    vmem = pl.BlockSpec(memory_space=pltpu.VMEM)
-    smem = pl.BlockSpec(memory_space=pltpu.SMEM)
     anywhere = pl.BlockSpec(memory_space=pl.ANY)
     sems = lambda *count: pltpu.SemaphoreType.DMA(count)
     out = pl.pallas_call(
         functools.partial(layer_kernel, sections, devices),
         out_shape=jax.ShapeDtypeStruct((sections, quarter, width), bf16),
-        in_specs=[smem] * 3 + [anywhere] * 14,
-        out_specs=vmem,
+        in_specs=[anywhere] * 17,
+        out_specs=anywhere,
         scratch_shapes=[
+            pltpu.SMEM(lengths.shape, jnp.int32),
+            pltpu.SMEM(expert_ids.shape[::-1], jnp.int32),
+            pltpu.SMEM(route_weights.shape[::-1], f32),
             pltpu.VMEM(hidden.shape, bf16),
             pltpu.VMEM((1, width), f32),
             pltpu.VMEM((1, latent), f32),
@@ -620,7 +676,7 @@
             pltpu.VMEM((row_count, width), f32),
             pltpu.VMEM((row_count, padded, latent), f32),
             pltpu.VMEM((row_count, padded, rope), f32),
-            pltpu.VMEM((row_count, padded, 128), f32),
+            pltpu.VMEM((row_count * padded, 128), f32),
             pltpu.VMEM((row_count * padded, slots_kept), f32),
             pltpu.VMEM((row_count, padded, latent), f32),
             pltpu.VMEM((sections, quarter, width), bf16),
@@ -630,11 +686,11 @@
             pltpu.VMEM((quarter, width), f32),
             pltpu.VMEM((quarter, 2 * experts), f32),
             pltpu.VMEM((total, quarter, 2 * experts), f32),
-            pltpu.VMEM((chunks, quarter, span), bf16),
-            pltpu.VMEM((chunks, 2, sections, pairs, quarter, span), bf16),
+            pltpu.VMEM((out_chunks, quarter, out_span), bf16),
+            pltpu.VMEM((out_chunks, 2, sections, pairs, quarter, out_span), bf16),
             pltpu.VMEM((rows, local * slots), bf16),
             pltpu.VMEM((rows, local * slots), bf16),
-            pltpu.VMEM((local * slots, span), bf16),
+            pltpu.VMEM((local * slots, out_span), bf16),
             pltpu.VMEM((local * slots, 2 * units), f32),
             pltpu.VMEM((local * slots, units), bf16),
             pltpu.VMEM((chunks, 2, sections, pairs, quarter, span), bf16),
@@ -645,7 +701,7 @@
             pltpu.VMEM((chunks, pairs, quarter, span), bf16),
             pltpu.VMEM((chunks, quarter, span), bf16),
             pltpu.VMEM((chunks, sections, quarter, span), bf16),
-            sems(10),
+            sems(13),
             sems(2 * groups),
             sems(local),
             sems(local),
@@ -653,20 +709,21 @@
             sems(sections),
             sems(total),
             sems(total),
+            sems(out_chunks, pairs),
+            sems(out_chunks, pairs),
+            sems(out_chunks, sections, pairs),
+            sems(out_chunks, sections, pairs),
+            sems(out_chunks),
+            sems(out_chunks),
+            sems(chunks),
+            sems(chunks),
+            sems(chunks, sections, pairs),
+            sems(chunks, sections, pairs),
             sems(chunks, pairs),
             sems(chunks, pairs),
             sems(chunks, sections),
             sems(chunks, sections),
             sems(chunks),
-            sems(chunks),
-            sems(chunks),
-            sems(chunks),
-            sems(chunks, sections),
-            sems(chunks, sections),
-            sems(chunks, pairs),
-            sems(chunks, pairs),
-            sems(chunks, sections),
-            sems(chunks, sections),
         ],
         compiler_params=pltpu.CompilerParams(
             collective_id=0, has_side_effects=True, vmem_limit_bytes=63 * 1024 * 1024

time: 61.2 us -> 57.8 us (0.944)
  Pallas kernels: 59.5 us -> 56.1 us
    pallas_call x1, Pallas kernels: 59.5 us -> 56.1 us  [per_device(): pl.pallas_call(functools.partial(layer_kernel, sections, devices), out_sh...]
where the time goes in v3:
time: 57.8 us; the launch traced here: 57.7 us
  Pallas kernels  56.1 us (97%)
  local copies, waits for them, and re-layouts  1.57 us (3%)
    pallas_call x1, Pallas kernels, per_device(): pl.pallas_call(functools.partial(layer_kernel, sections, devices), out_sh...  56.1 us
    unnamed x1, local copies, waits for them, and re-layouts  1.57 us

profile of v3, /device:TPU:0, one launch (start us, length us, event | category | flops | bytes accessed | tf_op | source)
XLA Modules:
  0.0 57.7 jit_solution(8431136149316575445)
XLA Ops:
  0.0 56.1 %shard_map.163 = bf16[4,8,2048]{2,1,0:T(8,128)(2,1)} custom-call(s32[32]{0:T(128)} %lengths_in.1, s32[6,32]{1,0:T(8,128)} %bitcast.9, f32[6,32]{1,0:T(8,128)} %bitcast.10, bf16[32,2048]{1,0:T(8,128)(2,1)} %hidden_ref.1, f32[1,2048]{1,0:T(1,128)} %bitcast.7, f32[1,512]{1,0:T(1,128)} %bitcast.11, f32[1,2048]{1,0:T(1,128)} %bitcast.8, ...), custom_call_target="tpu_custom_call" | custom-call | tf_op jit(solution)/shard_map/pallas_call | solution.py:655
  56.1 1.6 %copy.19 = bf16[32,2048]{1,0:T(8,128)(2,1)} copy(bf16[32,2048]{1,0:T(8,128)(2,1)} %bitcast.6) | data formatting | bytes 262144

commit v4 on v3

--- a/solution.py
+++ b/solution.py
@@ -220,12 +220,6 @@
     key_up_copy.start()
     latent_copy.start()
     rope_key_copy.start()
-    for g in range(groups):
-        for copy in cache_copies(g):
-            copy.start()
-    value_up_copy.start()
-    out_copy.start()
-
     barrier = pltpu.get_barrier_semaphore()
 
     @pl.loop(1, total)
@@ -250,6 +244,11 @@
     query_rope[...] = jnp.zeros_like(query_rope)
     self_scores[...] = jnp.zeros_like(self_scores)
     query_copy.wait()
+    for g in range(groups):
+        for copy in cache_copies(g):
+            copy.start()
+    value_up_copy.start()
+    out_copy.start()
     queries = jnp.dot(normed, w_query[...], preferred_element_type=f32).astype(bf16).astype(f32)
     rope_key_copy.wait()
     latent_copy.wait()
@@ -433,7 +432,7 @@
     weight_map = jnp.dot(known, weight_pick, preferred_element_type=f32)
     column = lax.broadcasted_iota(jnp.int32, (rows, wide), 1).astype(f32)
     chosen = slot_map == column - jnp.floor((column + 0.5) * (1.0 / slots)) * slots
-    pick[...] = jnp.where(chosen, 1.0, 0.0).astype(bf16)
+    pick[...] = jnp.where(chosen, 1.0, 0.0).astype(bf16).T
     mix[...] = jnp.where(chosen, weight_map, 0.0).astype(bf16)
 
     def to_partner(k):
@@ -451,9 +450,7 @@
             to_partner(k + 1)
         pair_copy(k, 1 - core).wait_recv()
         block = rows_all[k].astype(f32).reshape(rows, out_span).astype(bf16)
-        packed[...] = lax.dot_general(
-            pick[...], block, (((0,), (0,)), ((), ())), preferred_element_type=f32
-        ).astype(bf16)
+        packed[...] = jnp.dot(pick[...], block, preferred_element_type=f32).astype(bf16)
         for e in range(local):
             if k == 0:
                 up_copy(e).wait()
@@ -688,7 +685,7 @@
             pltpu.VMEM((total, quarter, 2 * experts), f32),
             pltpu.VMEM((out_chunks, quarter, out_span), bf16),
             pltpu.VMEM((out_chunks, 2, sections, pairs, quarter, out_span), bf16),
-            pltpu.VMEM((rows, local * slots), bf16),
+            pltpu.VMEM((local * slots, rows), bf16),
             pltpu.VMEM((rows, local * slots), bf16),
             pltpu.VMEM((local * slots, out_span), bf16),
             pltpu.VMEM((local * slots, 2 * units), f32),

time: 57.8 us -> 56.6 us (0.979)
  Pallas kernels: 56.1 us -> 54.9 us
    pallas_call x1, Pallas kernels: 56.1 us -> 54.9 us  [per_device(): pl.pallas_call(functools.partial(layer_kernel, sections, devices), out_sh...]
where the time goes in v4:
time: 56.6 us; the launch traced here: 56.5 us
  Pallas kernels  54.9 us (97%)
  local copies, waits for them, and re-layouts  1.57 us (3%)
    pallas_call x1, Pallas kernels, per_device(): pl.pallas_call(functools.partial(layer_kernel, sections, devices), out_sh...  54.9 us
    unnamed x1, local copies, waits for them, and re-layouts  1.57 us

profile of v4, /device:TPU:0, one launch (start us, length us, event | category | flops | bytes accessed | tf_op | source)
XLA Modules:
  0.0 56.5 jit_solution(8562673839360200511)
XLA Ops:
  0.0 54.9 %shard_map.163 = bf16[4,8,2048]{2,1,0:T(8,128)(2,1)} custom-call(s32[32]{0:T(128)} %lengths_in.1, s32[6,32]{1,0:T(8,128)} %bitcast.9, f32[6,32]{1,0:T(8,128)} %bitcast.10, bf16[32,2048]{1,0:T(8,128)(2,1)} %hidden_ref.1, f32[1,2048]{1,0:T(1,128)} %bitcast.7, f32[1,512]{1,0:T(1,128)} %bitcast.11, f32[1,2048]{1,0:T(1,128)} %bitcast.8, ...), custom_call_target="tpu_custom_call" | custom-call | tf_op jit(solution)/shard_map/pallas_call | solution.py:652
  54.9 1.6 %copy.19 = bf16[32,2048]{1,0:T(8,128)(2,1)} copy(bf16[32,2048]{1,0:T(8,128)(2,1)} %bitcast.6) | data formatting | bytes 262144

commit v5 on v4

--- a/solution.py
+++ b/solution.py
@@ -469,9 +469,9 @@
                 gate, lift = both[:, :units], both[:, units:]
                 activated[held, :] = (gate / (1.0 + jnp.exp(-gate)) * lift).astype(bf16)
 
-    def back_pair_copy(k, which):
+    def back_pair_copy(k):
         return remote(
-            sum_out.at[k, which], pair_in.at[k], back_pair_send.at[k], back_pair_recv.at[k], partner
+            sum_out.at[k], pair_in.at[k], back_pair_send.at[k], back_pair_recv.at[k], partner
         )
 
     def back_plane_copy(k, i, landing, slot):
@@ -504,8 +504,8 @@
         )
 
     def over_plane(k):
-        back_pair_copy(k, 1 - core).wait_recv()
-        pair_sum[k] = (sum_out[k, core].astype(f32) + pair_in[k].astype(f32)).astype(bf16)
+        back_pair_copy(k).wait_recv()
+        pair_sum[k] = (pair_sum[k].astype(f32) + pair_in[k].astype(f32)).astype(bf16)
 
         @pl.loop(1, pairs)
         def _(j):
@@ -550,9 +550,16 @@
                     activated[held, :], w_down[e, :, part_of], preferred_element_type=f32
                 ).astype(bf16)
             )
-        mixed = jnp.dot(mix[...], jnp.concatenate(outs, axis=0), preferred_element_type=f32)
-        sum_out[k] = mixed.reshape(2, sections, pairs, quarter, span).astype(bf16)
-        back_pair_copy(k, 1 - core).start()
+        routed = jnp.concatenate(outs, axis=0)
+
+        def mixed_rows(which):
+            held = pl.ds(pl.multiple_of(which * (rows // 2), rows // 2), rows // 2)
+            mixed = jnp.dot(mix[held, :], routed, preferred_element_type=f32)
+            return mixed.reshape(sections, pairs, quarter, span)
+
+        sum_out[k] = mixed_rows(1 - core).astype(bf16)
+        back_pair_copy(k).start()
+        pair_sum[k] = mixed_rows(core).astype(bf16)
         if k > 0:
             over_plane(k - 1)
     over_plane(chunks - 1)
@@ -607,7 +614,7 @@
 
         for i in range(1, sections):
             done_copy(k, i, section).wait_send()
-        back_pair_copy(k, 1 - core).wait_send()
+        back_pair_copy(k).wait_send()
         finish_copy(k).wait()
 
 
@@ -690,7 +697,7 @@
             pltpu.VMEM((local * slots, out_span), bf16),
             pltpu.VMEM((local * slots, 2 * units), f32),
             pltpu.VMEM((local * slots, units), bf16),
-            pltpu.VMEM((chunks, 2, sections, pairs, quarter, span), bf16),
+            pltpu.VMEM((chunks, sections, pairs, quarter, span), bf16),
             pltpu.VMEM((chunks, sections, pairs, quarter, span), bf16),
             pltpu.VMEM((chunks, sections, pairs, quarter, span), bf16),
             pltpu.VMEM((chunks, sections, pairs, quarter, span), bf16),

time: 56.6 us -> 56.8 us (level)
  no operation moved by 1% of the time
where the time goes in v5:
time: 56.8 us; the launch traced here: 56.7 us
  Pallas kernels  55.1 us (97%)
  local copies, waits for them, and re-layouts  1.57 us (3%)
    pallas_call x1, Pallas kernels, per_device(): pl.pallas_call(functools.partial(layer_kernel, sections, devices), out_sh...  55.1 us
    unnamed x1, local copies, waits for them, and re-layouts  1.57 us

profile of v5, /device:TPU:0, one launch (start us, length us, event | category | flops | bytes accessed | tf_op | source)
XLA Modules:
  0.0 56.7 jit_solution(13838956765664437395)
XLA Ops:
  0.0 55.1 %shard_map.163 = bf16[4,8,2048]{2,1,0:T(8,128)(2,1)} custom-call(s32[32]{0:T(128)} %lengths_in.1, s32[6,32]{1,0:T(8,128)} %bitcast.9, f32[6,32]{1,0:T(8,128)} %bitcast.10, bf16[32,2048]{1,0:T(8,128)(2,1)} %hidden_ref.1, f32[1,2048]{1,0:T(1,128)} %bitcast.7, f32[1,512]{1,0:T(1,128)} %bitcast.11, f32[1,2048]{1,0:T(1,128)} %bitcast.8, ...), custom_call_target="tpu_custom_call" | custom-call | tf_op jit(solution)/shard_map/pallas_call | solution.py:659
  55.1 1.6 %copy.19 = bf16[32,2048]{1,0:T(8,128)(2,1)} copy(bf16[32,2048]{1,0:T(8,128)(2,1)} %bitcast.6) | data formatting | bytes 262144
